TPU v7x, 32 devices: a whole 2x2x4 slice. The times are simulated.
32 devices in a mesh: tm: 4 (over y, core), feed: 8 (over z, x).
Axes of the slice: x: 2, y: 2, z: 4, core: 2. Of those that a mesh axis runs over, the one named last changes fastest.
Arguments:
- voltages: bfloat16 [12, 1024, 16384], P('tm', 'feed'), may hold values from -6 to 6
- pfb_taps: float32 [4, 16384], replicated, may hold values from 0.2 to 1
- feed_of_slot: int32 [1024], replicated, may hold values from 0 to 1023, each once
Outputs:
- beam_power: float32 [4, 1024, 8192], P('tm', None, 'feed')
Inputs may be any that keep to these rules, and one draw needn't show every extreme that they name: feed_of_slot[256 * r + j] is the feed at position j of cylinder r; every feed stands at exactly one position.
All inputs are finite; a program needn't handle non-finite values.
Results may differ from a plain program's by a relative error of at most 0.0052.
Values may be sent and summed in bfloat16 or wider, within the bound.
No kernel may reach another device: no remote copies, remote signals or barrier semaphores. Data moves between devices by JAX's collectives and lax.ppermute only.
A program may use at most 128 MiB of HBM per device.

v0:
```python
import math

import jax
import jax.numpy as jnp
from jax import lax
from jax.sharding import PartitionSpec as P

CYLINDERS = 4
COL_FEEDS = 256
SECTION_ONE = 128
SECTION_TWO = 128


def passed_along(array, axis, by):
    peers = lax.axis_size(axis)
    pairs = [(i, i + by) for i in range(peers) if 0 <= i + by < peers]
    return lax.ppermute(array, axis, pairs)


def tables(columns, row_count, period, factor):
    row_index = jnp.arange(row_count, dtype=jnp.int32)[:, None]
    col_index = jnp.arange(columns, dtype=jnp.int32)[None, :]
    angles = (row_index * col_index % period).astype(jnp.float32) * (2.0 * math.pi / period)
    return (jnp.cos(angles) * factor, -jnp.sin(angles) * factor)


def complex_table(part_re, part_im):
    upper = jnp.stack([part_re, -part_im], axis=1)
    lower = jnp.stack([part_im, part_re], axis=1)
    return jnp.stack([upper, lower], axis=1)


def tap_sum(weights, blocks, count):
    total = weights[0] * blocks[0:count].astype(jnp.float32)
    for tap_index in range(1, weights.shape[0]):
        total = total + weights[tap_index] * blocks[tap_index : tap_index + count].astype(
            jnp.float32
        )
    return total


def on_device(voltages, pfb_taps, feed_of_slot):
    spectra_here = voltages.shape[0]
    feeds_here = voltages.shape[1]
    weights = pfb_taps[:, None, None, :]
    arrived = passed_along(voltages, "tm", -1)
    extended = jnp.concatenate([voltages, arrived], axis=0)
    framed = tap_sum(weights, extended, spectra_here).astype(jnp.bfloat16)
    framed = framed.reshape(spectra_here, feeds_here, SECTION_ONE, SECTION_TWO)
    f32 = jnp.float32
    one_re, one_im = tables(SECTION_ONE, SECTION_ONE, SECTION_ONE, 1.0)
    one_both = jnp.concatenate([one_re, one_im], axis=0).astype(jnp.bfloat16)
    first = jnp.einsum("kn,sfnm->sfkm", one_both, framed, preferred_element_type=f32)
    first_re = first[:, :, :SECTION_ONE, :]
    first_im = first[:, :, SECTION_ONE:, :]
    twist_re, twist_im = tables(SECTION_TWO, SECTION_ONE, SECTION_ONE * SECTION_TWO, 1.0)
    factor = 1.0 / math.sqrt(SECTION_ONE * SECTION_TWO)
    turned = jnp.concatenate(
        [
            ((first_re * twist_re - first_im * twist_im) * factor).astype(jnp.bfloat16),
            ((first_re * twist_im + first_im * twist_re) * factor).astype(jnp.bfloat16),
        ],
        axis=-1,
    )
    two_re, two_im = tables(SECTION_TWO, SECTION_TWO // 2, SECTION_TWO, 1.0)
    two_table = (
        complex_table(two_re, two_im)
        .reshape(SECTION_TWO // 2, 2, 2 * SECTION_TWO)
        .astype(jnp.bfloat16)
    )
    spectrum = jnp.einsum("qem,sfkm->sfqek", two_table, turned, preferred_element_type=f32).astype(
        jnp.bfloat16
    )
    spectrum = spectrum.reshape(spectra_here, feeds_here, SECTION_TWO // 2, 2 * SECTION_ONE)
    col_re, col_im = tables(COL_FEEDS, COL_FEEDS, COL_FEEDS, 1.0 / math.sqrt(COL_FEEDS))
    col_table = complex_table(col_re, col_im).astype(jnp.bfloat16)
    cyl_re, cyl_im = tables(CYLINDERS, CYLINDERS, CYLINDERS, 1.0 / math.sqrt(CYLINDERS))
    cyl_table = complex_table(cyl_re, cyl_im)
    highest = lax.Precision.HIGHEST
    received = lax.all_to_all(spectrum, "feed", split_axis=2, concat_axis=1, tiled=True)
    spectra = received.shape[0]
    owned = received.shape[2]
    shape = (spectra, CYLINDERS, COL_FEEDS, owned, 2, SECTION_ONE)
    grid = jnp.take(received, feed_of_slot, axis=1).reshape(shape)
    along = jnp.einsum("pedj,scjqdk->scpqek", col_table, grid, preferred_element_type=f32)
    beam = jnp.einsum("medc,scpqdk->smpqek", cyl_table, along, precision=highest)
    energy = (
        beam[:, :, :, :, 0, :] * beam[:, :, :, :, 0, :]
        + beam[:, :, :, :, 1, :] * beam[:, :, :, :, 1, :]
    )
    powers = energy.reshape(spectra, CYLINDERS * COL_FEEDS, owned * SECTION_ONE)
    return jnp.sum(powers, axis=0, keepdims=True)


def solution(mesh):
    in_specs = (P("tm", "feed", None), P(), P())
    out_specs = P("tm", None, "feed")
    return jax.shard_map(
        on_device, mesh=mesh, in_specs=in_specs, out_specs=out_specs, check_vma=False
    )
```

profile of v0, /device:TPU:1, one launch (start us, length us, event | category | flops | bytes accessed | tf_op | source)
XLA Modules:
  0.0 577.1 jit_solution(629474096302529356)
XLA Ops:
  0.0 0.0 copy-start
  0.0 2.0 collective-permute-start
  2.1 0.3 fusion.43
  2.3 0.1 copy.57
  2.4 0.3 sine_negate_fusion
  2.7 0.1 copy.58
  2.8 0.1 fusion.46
  2.9 0.2 negate_convert_fusion.2
  3.3 0.3 negate_convert_fusion.1
  3.5 6.1 %constant_dynamic-update-slice_fusion.1 = bf16[6,128,16384]{2,1,0:T(8,128)(2,1)S(1)} fusion(bf16[3,128,16384]{2,1,0:T(8,128)(2,1)} %param.3), kind=kLoop, calls=%fused_computation.87 | loop fusion | bytes 25165824
  9.7 0.0 copy-done
  9.7 0.2 fusion.59
  9.9 131.2 %collective-permute-done = bf16[3,128,16384]{2,1,0:T(8,128)(2,1)} collective-permute-done((bf16[3,128,16384]{2,1,0:T(8,128)(2,1)}, bf16[3,128,16384]{2,1,0:T(8,128)(2,1)}, u32[]{:S(2)}, u32[]{:S(2)}) %collective-permute-start) | collective-permute-done | bytes 12582944 | tf_op jit(solution)/shard_map/ppermute | solution.py:17
  141.0 6.5 %constant_dynamic-update-slice_fusion = bf16[6,128,16384]{2,1,0:T(8,128)(2,1)S(1)} fusion(bf16[6,128,16384]{2,1,0:T(8,128)(2,1)S(1)} %constant_dynamic-update-slice_fusion.1, bf16[3,128,16384]{2,1,0:T(8,128)(2,1)} %collective-permute-done), kind=kLoop, calls=%fused_computation.86 | loop fusion | bytes 25165824 | tf_op jit(solution)/shard_map/concatenate | solution.py:47
  147.5 17.4 %add_convert_fusion = bf16[3,128,16384]{2,1,0:T(8,128)(2,1)} fusion(bf16[3,128,16384]{2,1,0:T(8,128)(2,1)} %collective-permute-done, bf16[3,128,16384]{2,1,0:T(8,128)(2,1)} %param.3, bf16[6,128,16384]{2,1,0:T(8,128)(2,1)S(1)} %constant_dynamic-update-slice_fusion, f32[16384]{0:T(1024)S(1)} %bitcast.93, f32[16384]{0:T(1024)S(1)} %bitcast.94, ...), kind=kLoop, calls=%fused_computation.8 | loop fusion | flops 75497472 | bytes 63176704 | tf_op jit(solution)/shard_map/convert_element_type | solution.py:48
  164.9 11.5 %copy.91 = bf16[48,8,128,128]{3,2,1,0:T(8,128)(2,1)} copy(bf16[48,8,128,128]{3,1,2,0:T(8,128)(2,1)} %bitcast.90) | data formatting | bytes 25165824
  176.4 21.7 %convolution_bitcast_fusion = f32[3,128,256,128]{2,3,1,0:T(8,128)} fusion(bf16[128,128]{1,0:T(8,128)(2,1)S(1)} %get-tuple-element.17, bf16[128,128]{1,0:T(8,128)(2,1)S(1)} %get-tuple-element.18, bf16[3,128,128,128]{3,2,1,0:T(8,128)(2,1)} %bitcast.86), kind=kOutput, calls=%fused_computation.1 | convolution fusion | flops 3221356544 | bytes 62980096 | tf_op jit(solution)/shard_map/kn,sfnm->sfkm/dot_general | solution.py:53
  198.1 25.5 %multiply_convert_fusion.1 = (bf16[3,128,128,128]{2,3,1,0:T(8,128)(2,1)}, bf16[3,128,128,128]{2,3,1,0:T(8,128)(2,1)}) fusion(f32[3,128,256,128]{2,3,1,0:T(8,128)} %convolution_bitcast_fusion, f32[128,128]{0,1:T(8,128)S(1)} %copy.58, f32[128,128]{0,1:T(8,128)S(1)} %copy.57), kind=kLoop, calls=%fused_computation.7 | loop fusion | flops 62914560 | bytes 75628544 | tf_op jit(solution)/shard_map/convert_element_type | solution.py:60
  223.6 14.7 %convert_bitcast_fusion = bf16[3,128,64,2,128]{4,2,3,1,0:T(8,128)(2,1)} fusion(bf16[3,128,128,128]{2,3,1,0:T(8,128)(2,1)} %get-tuple-element.6, bf16[3,128,128,128]{2,3,1,0:T(8,128)(2,1)} %get-tuple-element.5, bf16[64,1,256]{2,0,1:T(8,128)(2,1)S(1)} %stack.67, bf16[64,1,256]{2,0,1:T(8,128)(2,1)S(1)} %stack.65), kind=kOutput, calls=%fused_computation.18 | convolution fusion | flops 3277979648 | bytes 37814272 | tf_op jit(solution)/shard_map/qem,sfkm->sfqek/dot_general | solution.py:71
  238.3 0.0 copy-start.1
  238.3 17.6 %copy.85 = bf16[3,128,64,2,128]{1,4,3,0,2:T(8,128)(2,1)} copy(bf16[3,128,64,2,128]{4,2,3,1,0:T(8,128)(2,1)} %convert_bitcast_fusion) | data formatting | bytes 25165824 | tf_op jit(solution)/shard_map/reshape | solution.py:74
  255.9 5.5 all-to-all-start
  261.4 0.0 copy-done.1
  261.5 0.1 fusion.53
  261.5 0.1 negate_multiply_fusion.1
  261.6 1.0 fusion.22
  262.6 1.1 negate_convert_fusion
  263.8 154.2 %all-to-all-done = bf16[3,128,64,256]{1,3,0,2:T(8,128)(2,1)} async-done(((bf16[3,128,64,256]{1,3,0,2:T(8,128)(2,1)}), bf16[3,128,64,256]{1,3,0,2:T(8,128)(2,1)}, u32[]{:S(2)}, u32[]{:S(2)}) %all-to-all-start) | async-done | bytes 12582944 | tf_op jit(solution)/shard_map/all_to_all | solution.py:80
  418.0 17.4 %copy.65 = bf16[3,8,128,8,256]{4,3,2,1,0:T(8,128)(2,1)} copy(bf16[3,8,128,8,256]{2,4,0,3,1:T(8,128)(2,1)} %bitcast.15) | data formatting | bytes 25165824 | tf_op jit(solution)/shard_map/all_to_all | solution.py:80
  435.3 16.2 %gather_fusion = bf16[1024,3,8,256]{3,2,1,0:T(8,128)(2,1)} fusion(bf16[3,1024,8,256]{3,2,1,0:T(8,128)(2,1)} %bitcast.88, s32[1024]{0:T(1024)S(1)} %fusion.49), kind=kCustom, calls=%fused_computation | custom fusion | bytes 25169920 | tf_op jit(solution)/shard_map/jit(_take)/gather | solution.py:84
  451.5 16.8 %copy.66 = bf16[3,4,256,8,2,128]{2,5,4,3,1,0:T(8,128)(2,1)} copy(bf16[3,4,256,8,2,128]{5,3,4,0,2,1:T(8,128)(2,1)} %bitcast.89) | data formatting | bytes 25165824 | tf_op jit(solution)/shard_map/jit(_take)/gather | solution.py:84
  468.3 16.3 %fusion.10 = f32[3,4,256,8,2,128,1]{2,5,4,3,1,0,6:T(8,128)} fusion(bf16[3,4,256,8,2,128]{2,5,4,3,1,0:T(8,128)(2,1)} %copy.66, pred[4,256]{1,0:T(4,128)(4,1)S(1)} %broadcast_in_dim.13, bf16[256,1,2,256]{3,0,2,1:T(8,128)(2,1)S(1)} %get-tuple-element.12, bf16[256,1,2,256]{3,0,2,1:T(8,128)(2,1)S(1)} %get-tuple-element.11), kind=kOutput, calls=%fused_computation.20 | convolution fusion | flops 6449790976 | bytes 38274048 | tf_op jit(solution)/shard_map/pedj,scjqdk->scpqek/dot_general | solution.py:85
  484.6 30.0 %copy.80 = f32[3,4,256,8,2,128,1]{5,1,4,6,3,2,0:T(4,128)} copy(f32[3,4,256,8,2,128,1]{2,5,4,3,1,0,6:T(8,128)} %fusion.10) | data formatting | bytes 50331648 | tf_op jit(solution)/shard_map/pedj,scjqdk->scpqek/transpose | solution.py:85
  514.6 45.7 %convolution_bitcast_fusion.1 = f32[3,4,256,8,2,128]{5,1,4,3,2,0:T(4,128)S(1)} fusion(f32[3,4,256,8,2,128,1]{5,1,4,6,3,2,0:T(4,128)} %copy.80, f32[4,1,2,4]{3,0,2,1:T(4,128)S(1)} %get-tuple-element.16, f32[4,1,2,4]{3,0,2,1:T(4,128)S(1)} %get-tuple-element.15), kind=kOutput, calls=%fused_computation.9 | convolution fusion | flops 603979840 | bytes 50331904 | tf_op jit(solution)/shard_map/medc,scpqdk->smpqek/dot_general | solution.py:86
  560.3 9.6 %fusion.5 = f32[4,256,8,128]{3,0,2,1:T(4,128)S(1)} fusion(f32[3,4,256,8,2,128]{5,1,4,3,2,0:T(4,128)S(1)} %convolution_bitcast_fusion.1), kind=kLoop, calls=%fused_computation.13 | loop fusion | flops 11534336 | bytes 29360128 | tf_op jit(solution)/shard_map/reduce_sum | solution.py:92
  570.0 2.2 copy.72
  572.2 4.9 broadcast_in_dim.17
  (10 shorter events, 0.2 us)
Async XLA Ops:
  0.0 9.7 %copy-start = (f32[4,16384]{1,0:T(4,128)S(1)}, f32[4,16384]{1,0:T(4,128)}, u32[]{:S(2)}) copy-start(f32[4,16384]{1,0:T(4,128)} %param.4) | copy-start | bytes 786436
  0.0 141.0 %collective-permute-start = (bf16[3,128,16384]{2,1,0:T(8,128)(2,1)}, bf16[3,128,16384]{2,1,0:T(8,128)(2,1)}, u32[]{:S(2)}, u32[]{:S(2)}) collective-permute-start(bf16[3,128,16384]{2,1,0:T(8,128)(2,1)} %param.3), channel_id=1, source_target_pairs={{8,0},{16,8},{24,16},{9,1},{17,9},{25,17},{10,2},{18,10},{26,18},{... | collective-permute-start | bytes 37748744 | tf_op jit(solution)/shard_map/ppermute | solution.py:17
  238.3 23.1 %copy-start.1 = (s32[1024]{0:T(1024)S(1)}, s32[1024]{0:T(1024)}, u32[]{:S(2)}) copy-start(s32[1024]{0:T(1024)} %param.5) | copy-start | bytes 12292
  255.9 162.1 %all-to-all-start = ((bf16[3,128,64,256]{1,3,0,2:T(8,128)(2,1)}), bf16[3,128,64,256]{1,3,0,2:T(8,128)(2,1)}, u32[]{:S(2)}, u32[]{:S(2)}) async-start(bf16[3,128,64,256]{1,3,0,2:T(8,128)(2,1)} %bitcast.87), calls=%async_computation | async-start | bytes 25165824 | tf_op jit(solution)/shard_map/all_to_all | solution.py:80
where the time goes:
time: 579 us; the launch traced here: 577 us
  waiting for transfers between devices  285 us (49%)
  local copies, waits for them, and re-layouts  130 us (22%)
  matrix products  98.4 us (17%)
  other arithmetic  55.8 us (10%)
  starting transfers between devices  7.57 us (1%)
    all_to_all x1, waiting for transfers between devices, on_device(): lax.all_to_all(spectrum, 'feed', split_axis=2, concat_axis=1, tiled=True)  154 us
    ppermute x1, waiting for transfers between devices, passed_along(): return lax.ppermute(array, axis, pairs)  131 us
    dot_general x1, matrix products, on_device(): jnp.einsum('medc,scpqdk->smpqek', cyl_table, along, precision=highest)  45.7 us
    gather x2, local copies, waits for them, and re-layouts, on_device(): grid = jnp.take(received, feed_of_slot, axis=1).reshape(shape)  32.9 us
    transpose x1, local copies, waits for them, and re-layouts, on_device(): jnp.einsum('pedj,scjqdk->scpqek', col_table, grid, preferred_element_type...  30 us
    convert_element_type x1, other arithmetic, on_device(): ((first_re * twist_re - first_im * twist_im) * factor).astype(jnp.bfloat16)  25.5 us
    dot_general x1, matrix products, on_device(): jnp.einsum('kn,sfnm->sfkm', one_both, framed, preferred_element_type=f32)  21.7 us
    unnamed x6, local copies, waits for them, and re-layouts  17.6 us
  transfers between devices with their start and end apart: 2, of which 2 were waited for; matrix products, arithmetic and copies ran while one was open for 2% of the time, Pallas kernels for 0%

commit v1 on v0

v1 whole, which is shorter than its diff:
```python
import functools
import math

import jax
import jax.numpy as jnp
import numpy as np
from jax import lax
from jax.experimental import pallas as pl
from jax.experimental.pallas import tpu as pltpu
from jax.sharding import PartitionSpec as P


CYLINDERS = 4
COL_FEEDS = 256
SECTION_ONE = 128
SECTION_TWO = 128
KEPT = SECTION_TWO // 2
FEED_TILE = 16
VMEM_LIMIT = 67043328
F32 = jnp.float32
BF16 = jnp.bfloat16


def tables(columns, row_count, period, factor):
    turns = np.arange(row_count)[:, None] * np.arange(columns)[None, :] % period
    angles = turns * (2.0 * math.pi / period)
    return ((np.cos(angles) * factor).astype(np.float32), (-np.sin(angles) * factor).astype(np.float32))


def whole_spec(array):
    return pl.BlockSpec(
        array.shape, lambda *_: (0,) * array.ndim, pipeline_mode=pl.Buffered(1)
    )


def channel_kernel(shape, me, *refs):
    del me
    count = sum(shape)
    voltages, small, outs = refs[:count], refs[count : count + 5], refs[count + 5 : -2]
    taps, one, twist_re, twist_im, two = small
    filt, spec = refs[-2:]
    rows = FEED_TILE
    parts = max(shape)

    def fir_of(part):
        blocks, at = [], 0
        for held in shape:
            blocks.append(voltages[at + (part if held > 1 else 0)])
            at += held

        def fir(a, carry):
            lanes = pl.ds(pl.multiple_of(a * SECTION_TWO, SECTION_TWO), SECTION_TWO)
            total = None
            for tap_index, block in enumerate(blocks):
                weight = taps[pl.ds(tap_index, 1), lanes]
                term = weight * block[:, lanes].astype(F32)
                total = term if total is None else total + term
            filt[pl.ds(pl.multiple_of(a * rows, rows), rows), :] = total
            return carry

        lax.fori_loop(0, SECTION_ONE, fir, 0, unroll=8)

    if parts == 1:
        fir_of(0)
    else:
        share = pl.num_programs(0) // parts
        for part in range(parts):
            pl.when(pl.program_id(0) // share == part)(functools.partial(fir_of, part))

    def transform(pair, carry):
        feeds = (2 * pair, 2 * pair + 1)
        framed = jnp.concatenate(
            [filt[pl.ds(f, SECTION_ONE, stride=rows), :].astype(BF16) for f in feeds], axis=1
        )
        first = jnp.dot(one[...], framed, preferred_element_type=F32)
        turned = []
        for i in range(2):
            lanes = slice(i * SECTION_TWO, (i + 1) * SECTION_TWO)
            first_re = first[:SECTION_ONE, lanes]
            first_im = first[SECTION_ONE:, lanes]
            turned_re = first_re * twist_re[...] - first_im * twist_im[...]
            turned_im = first_re * twist_im[...] + first_im * twist_re[...]
            turned.append(
                jnp.concatenate([turned_re.astype(BF16), turned_im.astype(BF16)], axis=1)
            )
        turned = jnp.concatenate(turned, axis=0)
        spectrum = lax.dot_general(
            two[...], turned, (((1,), (1,)), ((), ())), preferred_element_type=F32
        )
        for i, f in enumerate(feeds):
            lanes = slice(i * SECTION_ONE, (i + 1) * SECTION_ONE)
            spec[pl.ds(f, 2 * KEPT, stride=rows), :] = spectrum[:, lanes]
        return carry

    lax.fori_loop(0, rows // 2, transform, 0, unroll=2)
    at = 0
    for out in outs:
        count = out.shape[0]
        piece = spec[at * rows : (at + count) * rows, :]
        out[...] = piece.reshape(count, rows, SECTION_ONE).astype(BF16)
        at += count


def channelize(sources, me, pfb_taps, one, twist_re, twist_im, two, tiles, counts):
    length = SECTION_ONE * SECTION_TWO

    def index(at, skip, limit, i, me):
        return (at, jnp.clip(i + skip, 0, limit), 0)

    specs, operands = [], []
    for held in sources:
        for array, at, skip in held:
            limit = array.shape[1] // FEED_TILE - 1
            specs.append(
                pl.BlockSpec((None, FEED_TILE, length), functools.partial(index, at, skip, limit))
            )
            operands.append(array)
    small = (pfb_taps, one, twist_re, twist_im)
    two_spec = pl.BlockSpec(
        (None,) + two.shape[1:], lambda i, me: (me[0], 0, 0), pipeline_mode=pl.Buffered(1)
    )
    feeds = tiles * FEED_TILE
    return pl.pallas_call(
        functools.partial(channel_kernel, tuple(len(held) for held in sources)),
        grid_spec=pltpu.PrefetchScalarGridSpec(
            num_scalar_prefetch=1,
            grid=(tiles,),
            in_specs=specs + [whole_spec(array) for array in small] + [two_spec],
            out_specs=[
                pl.BlockSpec((count, FEED_TILE, SECTION_ONE), lambda i, me: (0, i, 0))
                for count in counts
            ],
            scratch_shapes=[
                pltpu.VMEM((SECTION_ONE * FEED_TILE, SECTION_TWO), F32),
                pltpu.VMEM((2 * KEPT * FEED_TILE, SECTION_ONE), F32),
            ],
        ),
        out_shape=[jax.ShapeDtypeStruct((count, feeds, SECTION_ONE), BF16) for count in counts],
        compiler_params=pltpu.CompilerParams(
            dimension_semantics=("arbitrary",), vmem_limit_bytes=VMEM_LIMIT
        ),
        cost_estimate=pl.CostEstimate(
            flops=4 * feeds * 256 * 128 * 128,
            bytes_accessed=feeds * length * 2 * 5,
            transcendentals=0,
        ),
    )(me, *operands, *small, two)


def copy_kernel(source, out):
    out[...] = source[...]


def block_of(voltages, at, first, feeds):
    length = voltages.shape[2]
    rows = min(32, feeds)
    skip = first // rows
    return pl.pallas_call(
        copy_kernel,
        grid=(feeds // rows,),
        in_specs=[pl.BlockSpec((1, rows, length), lambda i: (at, i + skip, 0))],
        out_specs=pl.BlockSpec((1, rows, length), lambda i: (0, i, 0)),
        out_shape=jax.ShapeDtypeStruct((1, feeds, length), BF16),
        compiler_params=pltpu.CompilerParams(
            dimension_semantics=("arbitrary",), vmem_limit_bytes=VMEM_LIMIT
        ),
        cost_estimate=pl.CostEstimate(
            flops=0, bytes_accessed=4 * feeds * length, transcendentals=0
        ),
    )(voltages)


def beam_kernel(peers, parts, has_before, *refs):
    count = peers * parts
    arrived, table, out = refs[:count], refs[count], refs[-1]
    before = refs[count + 1] if has_before else None
    slots, lanes = table.shape[0], arrived[0].shape[2]
    for i in range(arrived[0].shape[0] // 2):
        real = jnp.concatenate([a[2 * i] for a in arrived], axis=0)
        imag = jnp.concatenate([a[2 * i + 1] for a in arrived], axis=0)
        data = jnp.concatenate(
            [jnp.concatenate([real, imag], axis=1), jnp.concatenate([-imag, real], axis=1)],
            axis=0,
        )
        at = slice(i * lanes, (i + 1) * lanes)
        step = 512
        for row in range(0, slots, step):
            beam = jnp.dot(table[row : row + step, :], data, preferred_element_type=F32)
            power = beam[:, :lanes] * beam[:, :lanes] + beam[:, lanes:] * beam[:, lanes:]
            if before is not None:
                power = power + before[row : row + step, at]
            out[row : row + step, at] = power


def form_beams(arrived, table, before, channels, first):
    peers, parts = len(arrived), len(arrived[0])
    rows, _, lanes = arrived[0][0].shape
    slots = table.shape[0]
    width = min(2, rows // 2)
    offset = first // width
    out_spec = pl.BlockSpec((slots, width * lanes), lambda i: (0, i + offset))
    operands = [piece for held in arrived for piece in held]
    in_specs = [
        pl.BlockSpec((2 * width, piece.shape[1], lanes), lambda i: (i, 0, 0)) for piece in operands
    ]
    in_specs.append(whole_spec(table))
    operands.append(table)
    aliases = {}
    if before is not None:
        in_specs.append(out_spec)
        operands.append(before)
        aliases = {len(operands) - 1: 0}
    steps = rows // (2 * width)
    return pl.pallas_call(
        functools.partial(beam_kernel, peers, parts, before is not None),
        grid=(steps,),
        in_specs=in_specs,
        out_specs=out_spec,
        out_shape=jax.ShapeDtypeStruct((slots, channels), F32),
        input_output_aliases=aliases,
        compiler_params=pltpu.CompilerParams(
            dimension_semantics=("arbitrary",), vmem_limit_bytes=24 << 20
        ),
        cost_estimate=pl.CostEstimate(
            flops=8 * slots * slots * steps * width * lanes,
            bytes_accessed=8 * slots * steps * width * lanes + 4 * slots * slots,
            transcendentals=0,
        ),
    )(*operands)


def table_kernel(feeds, me, feed_of_slot, waves, out):
    rows = out.shape[0]
    slots = feed_of_slot.shape[0]
    lanes = waves.shape[1]
    shift = COL_FEEDS.bit_length() - 1
    row = pl.program_id(0) * rows + lax.broadcasted_iota(jnp.int32, (rows, lanes), 0)
    p = row & (COL_FEEDS - 1)
    m = row >> shift
    cosine = jnp.broadcast_to(waves[0:1, :], (rows, lanes))
    sine = jnp.broadcast_to(waves[1:2, :], (rows, lanes))
    slot_index = lax.broadcasted_iota(jnp.int32, (slots, lanes), 0)
    lane = lax.broadcasted_iota(jnp.int32, (1, lanes), 1)
    for at in range(0, slots, lanes):
        place = at + lane
        feed = ((place // feeds) ^ me[0]) * feeds + place % feeds
        match = feed_of_slot[...] == feed
        slot = jnp.sum(jnp.where(match, slot_index, 0), axis=0, keepdims=True)
        slot = jnp.broadcast_to(slot, (rows, lanes))
        cylinder = slot >> shift
        turn = p * (slot & (COL_FEEDS - 1)) + m * cylinder * (COL_FEEDS // CYLINDERS)
        turn = turn & (COL_FEEDS - 1)
        index = turn & (lanes - 1)
        real = jnp.take_along_axis(cosine, index, axis=1)
        imag = jnp.take_along_axis(sine, index, axis=1)
        flip = turn >= lanes
        out[:, at : at + lanes] = jnp.where(flip, -real, real).astype(BF16)
        out[:, slots + at : slots + at + lanes] = jnp.where(flip, -imag, imag).astype(BF16)


def beam_table(feed_of_slot, me, feeds):
    slots = CYLINDERS * COL_FEEDS
    half = COL_FEEDS // 2
    factor = 1.0 / math.sqrt(COL_FEEDS) / math.sqrt(CYLINDERS)
    angles = np.arange(half) * (2.0 * math.pi / COL_FEEDS)
    waves = np.zeros((8, half), np.float32)
    waves[0] = np.cos(angles) * factor
    waves[1] = -np.sin(angles) * factor
    rows = 256
    column = feed_of_slot.reshape(slots, 1)
    return pl.pallas_call(
        functools.partial(table_kernel, feeds),
        grid_spec=pltpu.PrefetchScalarGridSpec(
            num_scalar_prefetch=1,
            grid=(slots // rows,),
            in_specs=[whole_spec(column), whole_spec(waves)],
            out_specs=pl.BlockSpec((rows, 2 * slots), lambda i, me: (i, 0)),
        ),
        out_shape=jax.ShapeDtypeStruct((slots, 2 * slots), BF16),
        compiler_params=pltpu.CompilerParams(
            dimension_semantics=("arbitrary",), vmem_limit_bytes=24 << 20
        ),
        cost_estimate=pl.CostEstimate(
            flops=40 * slots * slots, bytes_accessed=4 * slots * slots, transcendentals=0
        ),
    )(me, column, jnp.asarray(waves))


def on_device(voltages, pfb_taps, feed_of_slot):
    spectra_here = voltages.shape[0]
    feeds_here = voltages.shape[1]
    times = lax.axis_size("tm")
    peers = lax.axis_size("feed")
    owned = KEPT // peers
    half = feeds_here // 2
    pairs = [(i + 1, i) for i in range(times - 1)]
    halo = []
    for i in range(spectra_here):
        held = []
        spans = [(0, half), (half, half)] if i == 0 else [(0, feeds_here)]
        for first, count in spans:
            block = block_of(voltages, i, first, count)
            held.append((lax.ppermute(block, "tm", pairs), 0, -first // FEED_TILE))
        halo.append(held)
    me = lax.axis_index("feed").astype(jnp.int32).reshape(1)
    one = jnp.asarray(np.concatenate(tables(SECTION_ONE, SECTION_ONE, SECTION_ONE, 1.0))).astype(BF16)
    factor = 1.0 / math.sqrt(SECTION_ONE * SECTION_TWO)
    twist_re, twist_im = tables(SECTION_TWO, SECTION_ONE, SECTION_ONE * SECTION_TWO, factor)
    two_re, two_im = tables(SECTION_TWO, KEPT, SECTION_TWO, 1.0)
    two = np.stack(
        [
            np.concatenate([two_re, -two_im], axis=1),
            np.concatenate([two_im, two_re], axis=1),
        ],
        axis=1,
    ).reshape(peers, 2 * owned, 2 * SECTION_TWO)
    order = np.arange(peers)[:, None] ^ np.arange(peers)[None, :]
    two = two[order].reshape(peers, 2 * KEPT, 2 * SECTION_TWO).astype(BF16)
    table = beam_table(feed_of_slot, me, feeds_here)
    chunks = []
    for s in range(spectra_here):
        spans = [(0, half), (half, half)] if s == 0 else [(0, feeds_here)]
        gathered = [[] for _ in range(peers)]
        for part, (first, count) in enumerate(spans):
            sources = []
            for tap_index in range(pfb_taps.shape[0]):
                at = s + tap_index
                if at < spectra_here:
                    sources.append([(voltages, at, first // FEED_TILE)])
                elif s == 0:
                    sources.append([(halo[0][part][0], 0, 0)])
                else:
                    sources.append(halo[at - spectra_here])
            pieces = channelize(
                sources,
                me,
                pfb_taps,
                one,
                twist_re,
                twist_im,
                two,
                count // FEED_TILE,
                [2 * owned] * peers,
            )
            gathered[0].append(pieces[0])
            for j in reversed(range(1, peers)):
                gathered[j].append(
                    lax.ppermute(pieces[j], "feed", [(i, i ^ j) for i in range(peers)])
                )
        chunks.append(gathered)
    power = None
    for arrived in chunks:
        power = form_beams(arrived, table, power, owned * SECTION_ONE, 0)
    return power[None]


def solution(mesh):
    in_specs = (P("tm", "feed", None), P(), P())
    out_specs = P("tm", None, "feed")

    return jax.shard_map(
        on_device, mesh=mesh, in_specs=in_specs, out_specs=out_specs, check_vma=False
    )
```

time: 579 us -> 438 us (0.76)
  the two profiles are of different devices: /device:TPU:1 before, /device:TPU:12 now
where the time goes in v1:
time: 438 us
  waiting for transfers between devices  223 us (51%)
  Pallas kernels  144 us (33%)
  starting transfers between devices  63.4 us (14%)
  local copies, waits for them, and re-layouts  6.63 us (2%)
    ppermute x28, waiting for transfers between devices, on_device(): lax.ppermute(pieces[j], 'feed', [(i, i ^ j) for i in range(peers)])  119 us
    ppermute x4, waiting for transfers between devices, on_device(): held.append((lax.ppermute(block, 'tm', pairs), 0, -first // FEED_TILE))  104 us
    pallas_call x4, Pallas kernels, channelize(): pl.pallas_call(functools.partial(channel_kernel, tuple((len(held) for hel...  81.6 us
    ppermute x28, starting transfers between devices, on_device(): lax.ppermute(pieces[j], 'feed', [(i, i ^ j) for i in range(peers)])  55.2 us
    pallas_call x3, Pallas kernels, form_beams(): pl.pallas_call(functools.partial(beam_kernel, peers, parts, before is not...  34.9 us
    pallas_call x4, Pallas kernels, block_of(): pl.pallas_call(copy_kernel, grid=(feeds // rows,), in_specs=[pl.BlockSpec...  14.9 us
    pallas_call x1, Pallas kernels, beam_table(): pl.pallas_call(functools.partial(table_kernel, feeds), grid_spec=pltpu.Pr...  13.1 us
  transfers between devices with their start and end apart: 32, of which 14 were waited for; matrix products, arithmetic and copies ran while one was open for 0% of the time, Pallas kernels for 29%

profile of v1, /device:TPU:12, one launch (start us, length us, event | category | flops | bytes accessed | tf_op | source)
XLA Modules:
  0.0 437.9 jit_solution(15850354333317902981)
XLA Ops:
  0.0 4.7 %shard_map.84 = bf16[1,128,16384]{2,1,0:T(8,128)(2,1)} custom-call(bf16[3,128,16384]{2,1,0:T(8,128)(2,1)} %refs_2_.3), custom_call_target="tpu_custom_call" | custom-call | bytes 8388608 | tf_op jit(solution)/shard_map/pallas_call | solution.py:158
  4.7 1.9 collective-permute-start.2
  6.6 4.8 %shard_map.85 = bf16[1,128,16384]{2,1,0:T(8,128)(2,1)} custom-call(bf16[3,128,16384]{2,1,0:T(8,128)(2,1)} %refs_2_.3), custom_call_target="tpu_custom_call" | custom-call | bytes 8388608 | tf_op jit(solution)/shard_map/pallas_call | solution.py:158
  11.5 2.5 collective-permute-start.3
  14.0 2.7 shard_map.82
  16.7 1.9 collective-permute-start
  18.6 2.7 shard_map.83
  21.2 1.9 collective-permute-start.1
  23.2 97.2 %collective-permute-done.refs_1_.refs_2_.refs_3_ = bf16[1,64,16384]{2,1,0:T(8,128)(2,1)} collective-permute-done((bf16[1,64,16384]{2,1,0:T(8,128)(2,1)}, bf16[1,64,16384]{2,1,0:T(8,128)(2,1)}, u32[]{:S(2)}, u32[]{:S(2)}) %collective-permute-start) | collective-permute-done | bytes 2097184 | tf_op jit(solution)/shard_map/ppermute | solution.py:303
  120.4 14.3 %shard_map.89 = (bf16[16,64,128]{2,1,0:T(8,128)(2,1)}, bf16[16,64,128]{2,1,0:T(8,128)(2,1)}, bf16[16,64,128]{2,1,0:T(8,128)(2,1)}, bf16[16,64,128]{2,1,0:T(8,128...) custom-call(s32[1]{0:T(128)} %bitcast.me, ...), custom_call_target="tpu_custom_call" | custom-call | flops 1073741824 | bytes 10485760 | tf_op jit(solution)/shard_map/pallas_call | solution.py:123
  134.7 1.6 collective-permute-start.18
  136.3 6.6 %collective-permute-done.1.refs_2_.refs_3_ = bf16[1,64,16384]{2,1,0:T(8,128)(2,1)} collective-permute-done((bf16[1,64,16384]{2,1,0:T(8,128)(2,1)}, bf16[1,64,16384]{2,1,0:T(8,128)(2,1)}, u32[]{:S(2)}, u32[]{:S(2)}) %collective-permute-start.1) | collective-permute-done | bytes 2097184 | tf_op jit(solution)/shard_map/ppermute | solution.py:303
  142.8 14.4 %shard_map.90 = (bf16[16,64,128]{2,1,0:T(8,128)(2,1)}, bf16[16,64,128]{2,1,0:T(8,128)(2,1)}, bf16[16,64,128]{2,1,0:T(8,128)(2,1)}, bf16[16,64,128]{2,1,0:T(8,128...) custom-call(s32[1]{0:T(128)} %bitcast.me, ...), custom_call_target="tpu_custom_call" | custom-call | flops 1073741824 | bytes 10485760 | tf_op jit(solution)/shard_map/pallas_call | solution.py:123
  157.2 1.6 collective-permute-start.19
  158.8 0.5 collective-permute-start.20
  159.2 1.6 collective-permute-start.21
  160.8 3.1 collective-permute-done.19.refs_3_
  163.9 0.7 copy-done.5
  164.6 5.6 %collective-permute-start.22 = (bf16[16,64,128]{2,1,0:T(8,128)(2,1)}, bf16[16,64,128]{2,1,0:T(8,128)(2,1)S(1)}, u32[]{:S(2)}, u32[]{:S(2)}) collective-permute-start(bf16[16,64,128]{2,1,0:T(8,128)(2,1)} %get-tuple-element.59), channel_id=1, source_target_pairs={{0,3},{1,2},{2,1},{3,0},{4,7},{5,6},{6,5},{7,4},{8,11},{9,10},{10,... | collective-permute-start | bytes 786440 | tf_op jit(solution)/shard_map/ppermute | solution.py:348
  170.1 0.7 copy-done.7
  170.9 10.7 %collective-permute-done.21.refs_5_ = bf16[16,64,128]{2,1,0:T(8,128)(2,1)S(1)} collective-permute-done((bf16[16,64,128]{2,1,0:T(8,128)(2,1)}, bf16[16,64,128]{2,1,0:T(8,128)(2,1)S(1)}, u32[]{:S(2)}, u32[]{:S(2)}) %collective-permute-start.21) | collective-permute-done | bytes 262176 | tf_op jit(solution)/shard_map/ppermute | solution.py:348
  181.6 0.7 copy-done.9
  182.3 4.9 %collective-permute-done.22.refs_6_ = bf16[16,64,128]{2,1,0:T(8,128)(2,1)S(1)} collective-permute-done((bf16[16,64,128]{2,1,0:T(8,128)(2,1)}, bf16[16,64,128]{2,1,0:T(8,128)(2,1)S(1)}, u32[]{:S(2)}, u32[]{:S(2)}) %collective-permute-start.22) | collective-permute-done | bytes 262176 | tf_op jit(solution)/shard_map/ppermute | solution.py:348
  187.2 0.7 copy-done.11
  187.9 1.7 collective-permute-start.25
  189.6 1.4 collective-permute-done.23.refs_7_
  191.0 0.7 copy-done.13
  191.7 5.0 %collective-permute-start.26 = (bf16[16,64,128]{2,1,0:T(8,128)(2,1)}, bf16[16,64,128]{2,1,0:T(8,128)(2,1)}, u32[]{:S(2)}, u32[]{:S(2)}) collective-permute-start(bf16[16,64,128]{2,1,0:T(8,128)(2,1)} %get-tuple-element.63), channel_id=1, source_target_pairs={{0,5},{1,4},{2,7},{3,6},{4,1},{5,0},{6,3},{7,2},{8,13},{9,12},{10,... | collective-permute-start | bytes 786440 | tf_op jit(solution)/shard_map/ppermute | solution.py:348
  196.7 21.2 %collective-permute-done.24.refs_8_ = bf16[16,64,128]{2,1,0:T(8,128)(2,1)S(1)} collective-permute-done((bf16[16,64,128]{2,1,0:T(8,128)(2,1)}, bf16[16,64,128]{2,1,0:T(8,128)(2,1)S(1)}, u32[]{:S(2)}, u32[]{:S(2)}) %collective-permute-start.24) | collective-permute-done | bytes 262176 | tf_op jit(solution)/shard_map/ppermute | solution.py:348
  217.9 0.7 copy-done.15
  218.6 3.4 collective-permute-start.27
  222.0 26.6 %collective-permute-done.25.refs_9_ = bf16[16,64,128]{2,1,0:T(8,128)(2,1)S(1)} collective-permute-done((bf16[16,64,128]{2,1,0:T(8,128)(2,1)}, bf16[16,64,128]{2,1,0:T(8,128)(2,1)S(1)}, u32[]{:S(2)}, u32[]{:S(2)}) %collective-permute-start.25) | collective-permute-done | bytes 262176 | tf_op jit(solution)/shard_map/ppermute | solution.py:348
  248.6 0.7 copy-done.17
  249.3 0.1 collective-permute-start.28
  249.4 2.0 collective-permute-start.29
  251.4 26.4 %shard_map.88 = (bf16[16,128,128]{2,1,0:T(8,128)(2,1)}, bf16[16,128,128]{2,1,0:T(8,128)(2,1)}, bf16[16,128,128]{2,1,0:T(8,128)(2,1)}, bf16[16,128,128]{2,1,0:T(8...) custom-call(s32[1]{0:T(128)} %bitcast.me, ...), custom_call_target="tpu_custom_call" | custom-call | flops 2147483648 | bytes 20971520 | tf_op jit(solution)/shard_map/pallas_call | solution.py:123
  277.8 1.6 collective-permute-start.30
  279.4 26.4 %shard_map.86 = (bf16[16,128,128]{2,1,0:T(8,128)(2,1)}, bf16[16,128,128]{2,1,0:T(8,128)(2,1)}, bf16[16,128,128]{2,1,0:T(8,128)(2,1)}, bf16[16,128,128]{2,1,0:T(8...) custom-call(s32[1]{0:T(128)} %bitcast.me, ...), custom_call_target="tpu_custom_call" | custom-call | flops 2147483648 | bytes 20971520 | tf_op jit(solution)/shard_map/pallas_call | solution.py:123
  305.9 0.1 collective-permute-start.4
  305.9 6.5 %collective-permute-start.5 = (bf16[16,128,128]{2,1,0:T(8,128)(2,1)}, bf16[16,128,128]{2,1,0:T(8,128)(2,1)S(1)}, u32[]{:S(2)}, u32[]{:S(2)}) collective-permute-start(bf16[16,128,128]{2,1,0:T(8,128)(2,1)} %get-tuple-element.39), channel_id=1, source_target_pairs={{0,2},{1,3},{2,0},{3,1},{4,6},{5,7},{6,4},{7,5},{8,10},{9,11},{10,... | collective-permute-start | bytes 1572872 | tf_op jit(solution)/shard_map/ppermute | solution.py:348
  312.4 0.8 collective-permute-start.11
  313.2 0.1 collective-permute-start.12
  313.3 0.8 collective-permute-start.31
  314.1 0.9 copy.11.feed_of_slot
  315.0 0.7 copy-done
  315.8 13.1 %shard_map.87.refs_16_.refs_8_ = bf16[1024,2048]{1,0:T(8,128)(2,1)S(1)} custom-call(s32[1]{0:T(128)} %bitcast.me, s32[1024,1]{1,0:T(8,128)S(1)} %copy.11.feed_of_slot, f32[8,128]{1,0:T(8,128)S(1)} %copy-done), custom_call_target="tpu_custom_call" | custom-call | flops 41943040 | bytes 4194304 | tf_op jit(solution)/shard_map/pallas_call | solution.py:271
  328.9 4.3 collective-permute-start.13
  333.3 2.4 collective-permute-start.15
  335.7 1.9 collective-permute-start.16
  337.6 1.5 collective-permute-start.17
  339.2 11.6 %shard_map.91.refs_9_ = f32[1024,1024]{1,0:T(8,128)} custom-call(bf16[16,64,128]{2,1,0:T(8,128)(2,1)S(1)} %copy-done.3, bf16[16,64,128]{2,1,0:T(8,128)(2,1)S(1)} %copy-done.4, bf16[16,64,128]{2,1,0:T(8,128)(2,1)} %collective-permute-done.18.refs_2_, bf16[16,64,128]{2,1,0:T(8,128)(2,1)S(1)} %copy-done.6, bf16[16,64,128]{2,1,0:T(8,128)(2,1)S(1)} %copy-done.8, ...), custom_call_target="tpu_custom_call" | custom-call | flops 8589934592 | bytes 12582912 | tf_op jit(solution)/shard_map/pallas_call | solution.py:214
  350.8 2.0 collective-permute-start.6
  352.8 9.7 %collective-permute-done.14.refs_4_ = bf16[16,128,128]{2,1,0:T(8,128)(2,1)S(1)} collective-permute-done((bf16[16,128,128]{2,1,0:T(8,128)(2,1)S(1)}, bf16[16,128,128]{2,1,0:T(8,128)(2,1)S(1)}, u32[]{:S(2)}, u32[]{:S(2)}) %collective-permute-start.14) | collective-permute-done | bytes 524320 | tf_op jit(solution)/shard_map/ppermute | solution.py:348
  362.5 3.4 collective-permute-start.7
  365.9 7.8 %collective-permute-done.15.refs_5_ = bf16[16,128,128]{2,1,0:T(8,128)(2,1)S(1)} collective-permute-done((bf16[16,128,128]{2,1,0:T(8,128)(2,1)S(1)}, bf16[16,128,128]{2,1,0:T(8,128)(2,1)S(1)}, u32[]{:S(2)}, u32[]{:S(2)}) %collective-permute-start.15) | collective-permute-done | bytes 524320 | tf_op jit(solution)/shard_map/ppermute | solution.py:348
  373.7 4.3 collective-permute-start.8
  378.0 19.4 %collective-permute-done.16.refs_6_ = bf16[16,128,128]{2,1,0:T(8,128)(2,1)S(1)} collective-permute-done((bf16[16,128,128]{2,1,0:T(8,128)(2,1)S(1)}, bf16[16,128,128]{2,1,0:T(8,128)(2,1)S(1)}, u32[]{:S(2)}, u32[]{:S(2)}) %collective-permute-start.16) | collective-permute-done | bytes 524320 | tf_op jit(solution)/shard_map/ppermute | solution.py:348
  397.4 1.3 collective-permute-start.9
  398.7 5.1 %collective-permute-done.17.refs_7_ = bf16[16,128,128]{2,1,0:T(8,128)(2,1)S(1)} collective-permute-done((bf16[16,128,128]{2,1,0:T(8,128)(2,1)S(1)}, bf16[16,128,128]{2,1,0:T(8,128)(2,1)S(1)}, u32[]{:S(2)}, u32[]{:S(2)}) %collective-permute-start.17) | collective-permute-done | bytes 524320 | tf_op jit(solution)/shard_map/ppermute | solution.py:348
  403.8 1.4 collective-permute-start.10
  405.2 11.7 %shard_map.92.refs_9_ = f32[1024,1024]{1,0:T(8,128)} custom-call(bf16[16,128,128]{2,1,0:T(8,128)(2,1)S(1)} %copy-done.2, bf16[16,128,128]{2,1,0:T(8,128)(2,1)S(1)} %collective-permute-done.11.refs_1_, bf16[16,128,128]{2,1,0:T(8,128)(2,1)S(1)} %collective-permute-done.12.refs_2_, ...), custom_call_target="tpu_custom_call", output_to_operand_aliasing={{}: (9, {})} | custom-call | flops 8589934592 | bytes 12582912 | tf_op jit(solution)/shard_map/pallas_call | solution.py:214
  416.9 3.0 collective-permute-done.9.refs_6_
  419.9 6.4 %collective-permute-done.10.refs_7_ = bf16[16,128,128]{2,1,0:T(8,128)(2,1)S(1)} collective-permute-done((bf16[16,128,128]{2,1,0:T(8,128)(2,1)S(1)}, bf16[16,128,128]{2,1,0:T(8,128)(2,1)S(1)}, u32[]{:S(2)}, u32[]{:S(2)}) %collective-permute-start.10) | collective-permute-done | bytes 524320 | tf_op jit(solution)/shard_map/ppermute | solution.py:348
  426.3 11.6 %shard_map.93 = f32[1024,1024]{1,0:T(8,128)} custom-call(bf16[16,128,128]{2,1,0:T(8,128)(2,1)S(1)} %copy-done.1, bf16[16,128,128]{2,1,0:T(8,128)(2,1)S(1)} %collective-permute-done.4.refs_1_, bf16[16,128,128]{2,1,0:T(8,128)(2,1)S(1)} %collective-permute-done.5.refs_2_, ...), custom_call_target="tpu_custom_call", output_to_operand_aliasing={{}: (9, {})} | custom-call | flops 8589934592 | bytes 12582912 | tf_op jit(solution)/shard_map/pallas_call | solution.py:214
  (71 shorter events, 0.2 us)
Async XLA Ops:
  4.7 244.7 %collective-permute-start.2 = (bf16[1,128,16384]{2,1,0:T(8,128)(2,1)}, bf16[1,128,16384]{2,1,0:T(8,128)(2,1)}, u32[]{:S(2)}, u32[]{:S(2)}) collective-permute-start(bf16[1,128,16384]{2,1,0:T(8,128)(2,1)} %shard_map.84), channel_id=1, source_target_pairs={{8,0},{16,8},{24,16},{9,1},{17,9},{25,17},{10,2},{18,10},{26,18},{... | collective-permute-start | bytes 12582920 | tf_op jit(solution)/shard_map/ppermute | solution.py:303
  11.5 266.3 %collective-permute-start.3 = (bf16[1,128,16384]{2,1,0:T(8,128)(2,1)}, bf16[1,128,16384]{2,1,0:T(8,128)(2,1)}, u32[]{:S(2)}, u32[]{:S(2)}) collective-permute-start(bf16[1,128,16384]{2,1,0:T(8,128)(2,1)} %shard_map.85), channel_id=1, source_target_pairs={{8,0},{16,8},{24,16},{9,1},{17,9},{25,17},{10,2},{18,10},{26,18},{... | collective-permute-start | bytes 12582920 | tf_op jit(solution)/shard_map/ppermute | solution.py:303
  16.7 103.7 %collective-permute-start = (bf16[1,64,16384]{2,1,0:T(8,128)(2,1)}, bf16[1,64,16384]{2,1,0:T(8,128)(2,1)}, u32[]{:S(2)}, u32[]{:S(2)}) collective-permute-start(bf16[1,64,16384]{2,1,0:T(8,128)(2,1)} %shard_map.82), channel_id=1, source_target_pairs={{8,0},{16,8},{24,16},{9,1},{17,9},{25,17},{10,2},{18,10},{26,18},{... | collective-permute-start | bytes 6291464 | tf_op jit(solution)/shard_map/ppermute | solution.py:303
  21.2 121.6 %collective-permute-start.1 = (bf16[1,64,16384]{2,1,0:T(8,128)(2,1)}, bf16[1,64,16384]{2,1,0:T(8,128)(2,1)}, u32[]{:S(2)}, u32[]{:S(2)}) collective-permute-start(bf16[1,64,16384]{2,1,0:T(8,128)(2,1)} %shard_map.83), channel_id=1, source_target_pairs={{8,0},{16,8},{24,16},{9,1},{17,9},{25,17},{10,2},{18,10},{26,18},{... | collective-permute-start | bytes 6291464 | tf_op jit(solution)/shard_map/ppermute | solution.py:303
  134.7 24.5 %collective-permute-start.18 = (bf16[16,64,128]{2,1,0:T(8,128)(2,1)}, bf16[16,64,128]{2,1,0:T(8,128)(2,1)}, u32[]{:S(2)}, u32[]{:S(2)}) collective-permute-start(bf16[16,64,128]{2,1,0:T(8,128)(2,1)} %get-tuple-element.55), channel_id=1, source_target_pairs={{0,1},{1,0},{2,3},{3,2},{4,5},{5,4},{6,7},{7,6},{8,9},{9,8},{10,11... | collective-permute-start | bytes 786440 | tf_op jit(solution)/shard_map/ppermute | solution.py:348
  157.2 6.6 %collective-permute-start.19 = (bf16[16,64,128]{2,1,0:T(8,128)(2,1)}, bf16[16,64,128]{2,1,0:T(8,128)(2,1)S(1)}, u32[]{:S(2)}, u32[]{:S(2)}) collective-permute-start(bf16[16,64,128]{2,1,0:T(8,128)(2,1)} %get-tuple-element.56), channel_id=1, source_target_pairs={{0,1},{1,0},{2,3},{3,2},{4,5},{5,4},{6,7},{7,6},{8,9},{9,8},{10,11... | collective-permute-start | bytes 786440 | tf_op jit(solution)/shard_map/ppermute | solution.py:348
  158.8 11.4 %collective-permute-start.20 = (bf16[16,64,128]{2,1,0:T(8,128)(2,1)}, bf16[16,64,128]{2,1,0:T(8,128)(2,1)S(1)}, u32[]{:S(2)}, u32[]{:S(2)}) collective-permute-start(bf16[16,64,128]{2,1,0:T(8,128)(2,1)} %get-tuple-element.57), channel_id=1, source_target_pairs={{0,2},{1,3},{2,0},{3,1},{4,6},{5,7},{6,4},{7,5},{8,10},{9,11},{10,... | collective-permute-start | bytes 786440 | tf_op jit(solution)/shard_map/ppermute | solution.py:348
  159.2 22.3 %collective-permute-start.21 = (bf16[16,64,128]{2,1,0:T(8,128)(2,1)}, bf16[16,64,128]{2,1,0:T(8,128)(2,1)S(1)}, u32[]{:S(2)}, u32[]{:S(2)}) collective-permute-start(bf16[16,64,128]{2,1,0:T(8,128)(2,1)} %get-tuple-element.58), channel_id=1, source_target_pairs={{0,2},{1,3},{2,0},{3,1},{4,6},{5,7},{6,4},{7,5},{8,10},{9,11},{10,... | collective-permute-start | bytes 786440 | tf_op jit(solution)/shard_map/ppermute | solution.py:348
  163.9 0.7 copy-start.5
  164.6 22.6 %collective-permute-start.22 = (bf16[16,64,128]{2,1,0:T(8,128)(2,1)}, bf16[16,64,128]{2,1,0:T(8,128)(2,1)S(1)}, u32[]{:S(2)}, u32[]{:S(2)}) collective-permute-start(bf16[16,64,128]{2,1,0:T(8,128)(2,1)} %get-tuple-element.59), channel_id=1, source_target_pairs={{0,3},{1,2},{2,1},{3,0},{4,7},{5,6},{6,5},{7,4},{8,11},{9,10},{10,... | collective-permute-start | bytes 786440 | tf_op jit(solution)/shard_map/ppermute | solution.py:348
  170.1 0.7 copy-start.7
  170.9 20.1 %collective-permute-start.23 = (bf16[16,64,128]{2,1,0:T(8,128)(2,1)}, bf16[16,64,128]{2,1,0:T(8,128)(2,1)S(1)}, u32[]{:S(2)}, u32[]{:S(2)}) collective-permute-start(bf16[16,64,128]{2,1,0:T(8,128)(2,1)} %get-tuple-element.60), channel_id=1, source_target_pairs={{0,3},{1,2},{2,1},{3,0},{4,7},{5,6},{6,5},{7,4},{8,11},{9,10},{10,... | collective-permute-start | bytes 786440 | tf_op jit(solution)/shard_map/ppermute | solution.py:348
  181.6 0.7 copy-start.9
  182.3 35.6 %collective-permute-start.24 = (bf16[16,64,128]{2,1,0:T(8,128)(2,1)}, bf16[16,64,128]{2,1,0:T(8,128)(2,1)S(1)}, u32[]{:S(2)}, u32[]{:S(2)}) collective-permute-start(bf16[16,64,128]{2,1,0:T(8,128)(2,1)} %get-tuple-element.61), channel_id=1, source_target_pairs={{0,4},{1,5},{2,6},{3,7},{4,0},{5,1},{6,2},{7,3},{8,12},{9,13},{10,... | collective-permute-start | bytes 786440 | tf_op jit(solution)/shard_map/ppermute | solution.py:348
  187.2 0.7 copy-start.11
  187.9 60.7 %collective-permute-start.25 = (bf16[16,64,128]{2,1,0:T(8,128)(2,1)}, bf16[16,64,128]{2,1,0:T(8,128)(2,1)S(1)}, u32[]{:S(2)}, u32[]{:S(2)}) collective-permute-start(bf16[16,64,128]{2,1,0:T(8,128)(2,1)} %get-tuple-element.62), channel_id=1, source_target_pairs={{0,4},{1,5},{2,6},{3,7},{4,0},{5,1},{6,2},{7,3},{8,12},{9,13},{10,... | collective-permute-start | bytes 786440 | tf_op jit(solution)/shard_map/ppermute | solution.py:348
  191.0 0.7 copy-start.13
  191.7 114.1 %collective-permute-start.26 = (bf16[16,64,128]{2,1,0:T(8,128)(2,1)}, bf16[16,64,128]{2,1,0:T(8,128)(2,1)}, u32[]{:S(2)}, u32[]{:S(2)}) collective-permute-start(bf16[16,64,128]{2,1,0:T(8,128)(2,1)} %get-tuple-element.63), channel_id=1, source_target_pairs={{0,5},{1,4},{2,7},{3,6},{4,1},{5,0},{6,3},{7,2},{8,13},{9,12},{10,... | collective-permute-start | bytes 786440 | tf_op jit(solution)/shard_map/ppermute | solution.py:348
  217.9 0.7 copy-start.15
  218.6 87.3 %collective-permute-start.27 = (bf16[16,64,128]{2,1,0:T(8,128)(2,1)}, bf16[16,64,128]{2,1,0:T(8,128)(2,1)}, u32[]{:S(2)}, u32[]{:S(2)}) collective-permute-start(bf16[16,64,128]{2,1,0:T(8,128)(2,1)} %get-tuple-element.64), channel_id=1, source_target_pairs={{0,5},{1,4},{2,7},{3,6},{4,1},{5,0},{6,3},{7,2},{8,13},{9,12},{10,... | collective-permute-start | bytes 786440 | tf_op jit(solution)/shard_map/ppermute | solution.py:348
  248.6 0.7 copy-start.17
  249.3 63.1 %collective-permute-start.28 = (bf16[16,64,128]{2,1,0:T(8,128)(2,1)}, bf16[16,64,128]{2,1,0:T(8,128)(2,1)}, u32[]{:S(2)}, u32[]{:S(2)}) collective-permute-start(bf16[16,64,128]{2,1,0:T(8,128)(2,1)} %get-tuple-element.65), channel_id=1, source_target_pairs={{0,6},{1,7},{2,4},{3,5},{4,2},{5,3},{6,0},{7,1},{8,14},{9,15},{10,... | collective-permute-start | bytes 786440 | tf_op jit(solution)/shard_map/ppermute | solution.py:348
  249.4 63.8 %collective-permute-start.29 = (bf16[16,64,128]{2,1,0:T(8,128)(2,1)}, bf16[16,64,128]{2,1,0:T(8,128)(2,1)}, u32[]{:S(2)}, u32[]{:S(2)}) collective-permute-start(bf16[16,64,128]{2,1,0:T(8,128)(2,1)} %get-tuple-element.66), channel_id=1, source_target_pairs={{0,6},{1,7},{2,4},{3,5},{4,2},{5,3},{6,0},{7,1},{8,14},{9,15},{10,... | collective-permute-start | bytes 786440 | tf_op jit(solution)/shard_map/ppermute | solution.py:348
  277.8 35.5 %collective-permute-start.30 = (bf16[16,64,128]{2,1,0:T(8,128)(2,1)}, bf16[16,64,128]{2,1,0:T(8,128)(2,1)}, u32[]{:S(2)}, u32[]{:S(2)}) collective-permute-start(bf16[16,64,128]{2,1,0:T(8,128)(2,1)} %get-tuple-element.67), channel_id=1, source_target_pairs={{0,7},{1,6},{2,5},{3,4},{4,3},{5,2},{6,1},{7,0},{8,15},{9,14},{10,... | collective-permute-start | bytes 786440 | tf_op jit(solution)/shard_map/ppermute | solution.py:348
  305.8 33.2 %copy-start.3 = (bf16[16,64,128]{2,1,0:T(8,128)(2,1)S(1)}, bf16[16,64,128]{2,1,0:T(8,128)(2,1)}, u32[]{:S(2)}) copy-start(bf16[16,64,128]{2,1,0:T(8,128)(2,1)} %get-tuple-element.53.refs_0_) | copy-start | bytes 786436
  305.8 33.2 %copy-start.4 = (bf16[16,64,128]{2,1,0:T(8,128)(2,1)S(1)}, bf16[16,64,128]{2,1,0:T(8,128)(2,1)}, u32[]{:S(2)}) copy-start(bf16[16,64,128]{2,1,0:T(8,128)(2,1)} %get-tuple-element.54.refs_1_) | copy-start | bytes 786436
  305.9 27.3 %collective-permute-start.4 = (bf16[16,128,128]{2,1,0:T(8,128)(2,1)}, bf16[16,128,128]{2,1,0:T(8,128)(2,1)S(1)}, u32[]{:S(2)}, u32[]{:S(2)}) collective-permute-start(bf16[16,128,128]{2,1,0:T(8,128)(2,1)} %get-tuple-element.38), channel_id=1, source_target_pairs={{0,1},{1,0},{2,3},{3,2},{4,5},{5,4},{6,7},{7,6},{8,9},{9,8},{10,11... | collective-permute-start | bytes 1572872 | tf_op jit(solution)/shard_map/ppermute | solution.py:348
  305.9 27.3 %collective-permute-start.5 = (bf16[16,128,128]{2,1,0:T(8,128)(2,1)}, bf16[16,128,128]{2,1,0:T(8,128)(2,1)S(1)}, u32[]{:S(2)}, u32[]{:S(2)}) collective-permute-start(bf16[16,128,128]{2,1,0:T(8,128)(2,1)} %get-tuple-element.39), channel_id=1, source_target_pairs={{0,2},{1,3},{2,0},{3,1},{4,6},{5,7},{6,4},{7,5},{8,10},{9,11},{10,... | collective-permute-start | bytes 1572872 | tf_op jit(solution)/shard_map/ppermute | solution.py:348
  312.4 23.2 %collective-permute-start.11 = (bf16[16,128,128]{2,1,0:T(8,128)(2,1)}, bf16[16,128,128]{2,1,0:T(8,128)(2,1)S(1)}, u32[]{:S(2)}, u32[]{:S(2)}) collective-permute-start(bf16[16,128,128]{2,1,0:T(8,128)(2,1)} %get-tuple-element.46), channel_id=1, source_target_pairs={{0,1},{1,0},{2,3},{3,2},{4,5},{5,4},{6,7},{7,6},{8,9},{9,8},{10,11... | collective-permute-start | bytes 1572872 | tf_op jit(solution)/shard_map/ppermute | solution.py:348
  313.2 24.3 %collective-permute-start.12 = (bf16[16,128,128]{2,1,0:T(8,128)(2,1)}, bf16[16,128,128]{2,1,0:T(8,128)(2,1)S(1)}, u32[]{:S(2)}, u32[]{:S(2)}) collective-permute-start(bf16[16,128,128]{2,1,0:T(8,128)(2,1)} %get-tuple-element.47), channel_id=1, source_target_pairs={{0,2},{1,3},{2,0},{3,1},{4,6},{5,7},{6,4},{7,5},{8,10},{9,11},{10,... | collective-permute-start | bytes 1572872 | tf_op jit(solution)/shard_map/ppermute | solution.py:348
  313.3 15.6 %collective-permute-start.31 = (bf16[16,64,128]{2,1,0:T(8,128)(2,1)}, bf16[16,64,128]{2,1,0:T(8,128)(2,1)S(1)}, u32[]{:S(2)}, u32[]{:S(2)}) collective-permute-start(bf16[16,64,128]{2,1,0:T(8,128)(2,1)} %get-tuple-element.68), channel_id=1, source_target_pairs={{0,7},{1,6},{2,5},{3,4},{4,3},{5,2},{6,1},{7,0},{8,15},{9,14},{10,... | collective-permute-start | bytes 786440 | tf_op jit(solution)/shard_map/ppermute | solution.py:348
  315.0 0.7 copy-start
  315.7 13.2 %copy-start.28 = (bf16[16,128,128]{2,1,0:T(8,128)(2,1)S(1)}, bf16[16,128,128]{2,1,0:T(8,128)(2,1)}, u32[]{:S(2)}) copy-start(bf16[16,128,128]{2,1,0:T(8,128)(2,1)} %get-tuple-element.48) | copy-start | bytes 1572868
  315.7 17.5 %copy-start.27 = (bf16[16,128,128]{2,1,0:T(8,128)(2,1)S(1)}, bf16[16,128,128]{2,1,0:T(8,128)(2,1)}, u32[]{:S(2)}) copy-start(bf16[16,128,128]{2,1,0:T(8,128)(2,1)} %get-tuple-element.49) | copy-start | bytes 1572868
  315.7 17.5 %copy-start.26 = (bf16[16,128,128]{2,1,0:T(8,128)(2,1)S(1)}, bf16[16,128,128]{2,1,0:T(8,128)(2,1)}, u32[]{:S(2)}) copy-start(bf16[16,128,128]{2,1,0:T(8,128)(2,1)} %get-tuple-element.50) | copy-start | bytes 1572868
  315.7 19.9 %copy-start.25 = (bf16[16,128,128]{2,1,0:T(8,128)(2,1)S(1)}, bf16[16,128,128]{2,1,0:T(8,128)(2,1)}, u32[]{:S(2)}) copy-start(bf16[16,128,128]{2,1,0:T(8,128)(2,1)} %get-tuple-element.51) | copy-start | bytes 1572868
  315.7 21.8 %copy-start.24 = (bf16[16,128,128]{2,1,0:T(8,128)(2,1)S(1)}, bf16[16,128,128]{2,1,0:T(8,128)(2,1)}, u32[]{:S(2)}) copy-start(bf16[16,128,128]{2,1,0:T(8,128)(2,1)} %get-tuple-element.52) | copy-start | bytes 1572868
  315.7 23.3 %copy-start.6 = (bf16[16,64,128]{2,1,0:T(8,128)(2,1)S(1)}, bf16[16,64,128]{2,1,0:T(8,128)(2,1)}, u32[]{:S(2)}) copy-start(bf16[16,64,128]{2,1,0:T(8,128)(2,1)} %copy-done.5) | copy-start | bytes 786436
  315.7 23.3 %copy-start.8 = (bf16[16,64,128]{2,1,0:T(8,128)(2,1)S(1)}, bf16[16,64,128]{2,1,0:T(8,128)(2,1)}, u32[]{:S(2)}) copy-start(bf16[16,64,128]{2,1,0:T(8,128)(2,1)} %copy-done.7) | copy-start | bytes 786436
  315.7 23.3 %copy-start.10 = (bf16[16,64,128]{2,1,0:T(8,128)(2,1)S(1)}, bf16[16,64,128]{2,1,0:T(8,128)(2,1)}, u32[]{:S(2)}) copy-start(bf16[16,64,128]{2,1,0:T(8,128)(2,1)} %copy-done.9) | copy-start | bytes 786436
  315.8 23.3 %copy-start.12 = (bf16[16,64,128]{2,1,0:T(8,128)(2,1)S(1)}, bf16[16,64,128]{2,1,0:T(8,128)(2,1)}, u32[]{:S(2)}) copy-start(bf16[16,64,128]{2,1,0:T(8,128)(2,1)} %copy-done.11) | copy-start | bytes 786436
  315.8 23.3 %copy-start.14 = (bf16[16,64,128]{2,1,0:T(8,128)(2,1)S(1)}, bf16[16,64,128]{2,1,0:T(8,128)(2,1)}, u32[]{:S(2)}) copy-start(bf16[16,64,128]{2,1,0:T(8,128)(2,1)} %copy-done.13) | copy-start | bytes 786436
  315.8 23.3 %copy-start.16 = (bf16[16,64,128]{2,1,0:T(8,128)(2,1)S(1)}, bf16[16,64,128]{2,1,0:T(8,128)(2,1)}, u32[]{:S(2)}) copy-start(bf16[16,64,128]{2,1,0:T(8,128)(2,1)} %copy-done.15) | copy-start | bytes 786436
  315.8 23.3 %copy-start.18 = (bf16[16,64,128]{2,1,0:T(8,128)(2,1)S(1)}, bf16[16,64,128]{2,1,0:T(8,128)(2,1)}, u32[]{:S(2)}) copy-start(bf16[16,64,128]{2,1,0:T(8,128)(2,1)} %copy-done.17) | copy-start | bytes 786436
  328.9 21.9 %collective-permute-start.13 = (bf16[16,128,128]{2,1,0:T(8,128)(2,1)S(1)}, bf16[16,128,128]{2,1,0:T(8,128)(2,1)S(1)}, u32[]{:S(2)}, u32[]{:S(2)}) collective-permute-start(bf16[16,128,128]{2,1,0:T(8,128)(2,1)S(1)} %copy-done.28), channel_id=1, source_target_pairs={{0,3},{1,2},{2,1},{3,0},{4,7},{5,6},{6,5},{7,4},{8,11},{9,10},{10,... | collective-permute-start | bytes 1572872 | tf_op jit(solution)/shard_map/ppermute | solution.py:348
  333.2 29.3 %collective-permute-start.14 = (bf16[16,128,128]{2,1,0:T(8,128)(2,1)S(1)}, bf16[16,128,128]{2,1,0:T(8,128)(2,1)S(1)}, u32[]{:S(2)}, u32[]{:S(2)}) collective-permute-start(bf16[16,128,128]{2,1,0:T(8,128)(2,1)S(1)} %copy-done.27), channel_id=1, source_target_pairs={{0,4},{1,5},{2,6},{3,7},{4,0},{5,1},{6,2},{7,3},{8,12},{9,13},{10,... | collective-permute-start | bytes 1572872 | tf_op jit(solution)/shard_map/ppermute | solution.py:348
  333.3 40.5 %collective-permute-start.15 = (bf16[16,128,128]{2,1,0:T(8,128)(2,1)S(1)}, bf16[16,128,128]{2,1,0:T(8,128)(2,1)S(1)}, u32[]{:S(2)}, u32[]{:S(2)}) collective-permute-start(bf16[16,128,128]{2,1,0:T(8,128)(2,1)S(1)} %copy-done.26), channel_id=1, source_target_pairs={{0,5},{1,4},{2,7},{3,6},{4,1},{5,0},{6,3},{7,2},{8,13},{9,12},{10,... | collective-permute-start | bytes 1572872 | tf_op jit(solution)/shard_map/ppermute | solution.py:348
  335.7 61.7 %collective-permute-start.16 = (bf16[16,128,128]{2,1,0:T(8,128)(2,1)S(1)}, bf16[16,128,128]{2,1,0:T(8,128)(2,1)S(1)}, u32[]{:S(2)}, u32[]{:S(2)}) collective-permute-start(bf16[16,128,128]{2,1,0:T(8,128)(2,1)S(1)} %copy-done.25), channel_id=1, source_target_pairs={{0,6},{1,7},{2,4},{3,5},{4,2},{5,3},{6,0},{7,1},{8,14},{9,15},{10,... | collective-permute-start | bytes 1572872 | tf_op jit(solution)/shard_map/ppermute | solution.py:348
  337.6 66.2 %collective-permute-start.17 = (bf16[16,128,128]{2,1,0:T(8,128)(2,1)S(1)}, bf16[16,128,128]{2,1,0:T(8,128)(2,1)S(1)}, u32[]{:S(2)}, u32[]{:S(2)}) collective-permute-start(bf16[16,128,128]{2,1,0:T(8,128)(2,1)S(1)} %copy-done.24), channel_id=1, source_target_pairs={{0,7},{1,6},{2,5},{3,4},{4,3},{5,2},{6,1},{7,0},{8,15},{9,14},{10,... | collective-permute-start | bytes 1572872 | tf_op jit(solution)/shard_map/ppermute | solution.py:348
  339.1 11.7 %copy-start.23 = (bf16[16,128,128]{2,1,0:T(8,128)(2,1)S(1)}, bf16[16,128,128]{2,1,0:T(8,128)(2,1)}, u32[]{:S(2)}) copy-start(bf16[16,128,128]{2,1,0:T(8,128)(2,1)} %get-tuple-element.40) | copy-start | bytes 1572868
  339.1 23.4 %copy-start.22 = (bf16[16,128,128]{2,1,0:T(8,128)(2,1)S(1)}, bf16[16,128,128]{2,1,0:T(8,128)(2,1)}, u32[]{:S(2)}) copy-start(bf16[16,128,128]{2,1,0:T(8,128)(2,1)} %get-tuple-element.41) | copy-start | bytes 1572868
  339.1 34.6 %copy-start.21 = (bf16[16,128,128]{2,1,0:T(8,128)(2,1)S(1)}, bf16[16,128,128]{2,1,0:T(8,128)(2,1)}, u32[]{:S(2)}) copy-start(bf16[16,128,128]{2,1,0:T(8,128)(2,1)} %get-tuple-element.42) | copy-start | bytes 1572868
  339.2 58.2 %copy-start.20 = (bf16[16,128,128]{2,1,0:T(8,128)(2,1)S(1)}, bf16[16,128,128]{2,1,0:T(8,128)(2,1)}, u32[]{:S(2)}) copy-start(bf16[16,128,128]{2,1,0:T(8,128)(2,1)} %get-tuple-element.43) | copy-start | bytes 1572868
  339.2 64.6 %copy-start.19 = (bf16[16,128,128]{2,1,0:T(8,128)(2,1)S(1)}, bf16[16,128,128]{2,1,0:T(8,128)(2,1)}, u32[]{:S(2)}) copy-start(bf16[16,128,128]{2,1,0:T(8,128)(2,1)} %get-tuple-element.44) | copy-start | bytes 1572868
  339.2 66.0 %copy-start.2 = (bf16[16,128,128]{2,1,0:T(8,128)(2,1)S(1)}, bf16[16,128,128]{2,1,0:T(8,128)(2,1)}, u32[]{:S(2)}) copy-start(bf16[16,128,128]{2,1,0:T(8,128)(2,1)} %get-tuple-element.45.refs_0_) | copy-start | bytes 1572868
  350.8 66.1 %collective-permute-start.6 = (bf16[16,128,128]{2,1,0:T(8,128)(2,1)S(1)}, bf16[16,128,128]{2,1,0:T(8,128)(2,1)S(1)}, u32[]{:S(2)}, u32[]{:S(2)}) collective-permute-start(bf16[16,128,128]{2,1,0:T(8,128)(2,1)S(1)} %copy-done.23), channel_id=1, source_target_pairs={{0,3},{1,2},{2,1},{3,0},{4,7},{5,6},{6,5},{7,4},{8,11},{9,10},{10,... | collective-permute-start | bytes 1572872 | tf_op jit(solution)/shard_map/ppermute | solution.py:348
  362.5 54.4 %collective-permute-start.7 = (bf16[16,128,128]{2,1,0:T(8,128)(2,1)S(1)}, bf16[16,128,128]{2,1,0:T(8,128)(2,1)S(1)}, u32[]{:S(2)}, u32[]{:S(2)}) collective-permute-start(bf16[16,128,128]{2,1,0:T(8,128)(2,1)S(1)} %copy-done.22), channel_id=1, source_target_pairs={{0,4},{1,5},{2,6},{3,7},{4,0},{5,1},{6,2},{7,3},{8,12},{9,13},{10,... | collective-permute-start | bytes 1572872 | tf_op jit(solution)/shard_map/ppermute | solution.py:348
  373.7 43.2 %collective-permute-start.8 = (bf16[16,128,128]{2,1,0:T(8,128)(2,1)S(1)}, bf16[16,128,128]{2,1,0:T(8,128)(2,1)S(1)}, u32[]{:S(2)}, u32[]{:S(2)}) collective-permute-start(bf16[16,128,128]{2,1,0:T(8,128)(2,1)S(1)} %copy-done.21), channel_id=1, source_target_pairs={{0,5},{1,4},{2,7},{3,6},{4,1},{5,0},{6,3},{7,2},{8,13},{9,12},{10,... | collective-permute-start | bytes 1572872 | tf_op jit(solution)/shard_map/ppermute | solution.py:348
  397.4 22.5 %collective-permute-start.9 = (bf16[16,128,128]{2,1,0:T(8,128)(2,1)S(1)}, bf16[16,128,128]{2,1,0:T(8,128)(2,1)S(1)}, u32[]{:S(2)}, u32[]{:S(2)}) collective-permute-start(bf16[16,128,128]{2,1,0:T(8,128)(2,1)S(1)} %copy-done.20), channel_id=1, source_target_pairs={{0,6},{1,7},{2,4},{3,5},{4,2},{5,3},{6,0},{7,1},{8,14},{9,15},{10,... | collective-permute-start | bytes 1572872 | tf_op jit(solution)/shard_map/ppermute | solution.py:348
  403.8 22.5 %collective-permute-start.10 = (bf16[16,128,128]{2,1,0:T(8,128)(2,1)S(1)}, bf16[16,128,128]{2,1,0:T(8,128)(2,1)S(1)}, u32[]{:S(2)}, u32[]{:S(2)}) collective-permute-start(bf16[16,128,128]{2,1,0:T(8,128)(2,1)S(1)} %copy-done.19), channel_id=1, source_target_pairs={{0,7},{1,6},{2,5},{3,4},{4,3},{5,2},{6,1},{7,0},{8,15},{9,14},{10,... | collective-permute-start | bytes 1572872 | tf_op jit(solution)/shard_map/ppermute | solution.py:348
  405.2 21.0 %copy-start.1 = (bf16[16,128,128]{2,1,0:T(8,128)(2,1)S(1)}, bf16[16,128,128]{2,1,0:T(8,128)(2,1)}, u32[]{:S(2)}) copy-start(bf16[16,128,128]{2,1,0:T(8,128)(2,1)} %get-tuple-element.37.refs_0_) | copy-start | bytes 1572868

commit v2 on v1

--- a/solution.py
+++ b/solution.py
@@ -33,39 +33,17 @@
     )
 
 
-def channel_kernel(shape, me, *refs):
+def channel_kernel(me, v0, v1, v2, v3, taps, one, twist_re, twist_im, two, *rest):
     del me
-    count = sum(shape)
-    voltages, small, outs = refs[:count], refs[count : count + 5], refs[count + 5 : -2]
-    taps, one, twist_re, twist_im, two = small
-    filt, spec = refs[-2:]
+    outs, (filt, spec) = rest[:-2], rest[-2:]
     rows = FEED_TILE
-    parts = max(shape)
-
-    def fir_of(part):
-        blocks, at = [], 0
-        for held in shape:
-            blocks.append(voltages[at + (part if held > 1 else 0)])
-            at += held
-
-        def fir(a, carry):
-            lanes = pl.ds(pl.multiple_of(a * SECTION_TWO, SECTION_TWO), SECTION_TWO)
-            total = None
-            for tap_index, block in enumerate(blocks):
-                weight = taps[pl.ds(tap_index, 1), lanes]
-                term = weight * block[:, lanes].astype(F32)
-                total = term if total is None else total + term
-            filt[pl.ds(pl.multiple_of(a * rows, rows), rows), :] = total
-            return carry
-
-        lax.fori_loop(0, SECTION_ONE, fir, 0, unroll=8)
-
-    if parts == 1:
-        fir_of(0)
-    else:
-        share = pl.num_programs(0) // parts
-        for part in range(parts):
-            pl.when(pl.program_id(0) // share == part)(functools.partial(fir_of, part))
+    for a in range(SECTION_ONE):
+        lanes = slice(a * SECTION_TWO, (a + 1) * SECTION_TWO)
+        total = None
+        for tap_index, block in enumerate((v0, v1, v2, v3)):
+            term = taps[tap_index : tap_index + 1, lanes] * block[:, lanes].astype(F32)
+            total = term if total is None else total + term
+        filt[a * rows : (a + 1) * rows, :] = total
 
     def transform(pair, carry):
         feeds = (2 * pair, 2 * pair + 1)
@@ -92,7 +70,7 @@
             spec[pl.ds(f, 2 * KEPT, stride=rows), :] = spectrum[:, lanes]
         return carry
 
-    lax.fori_loop(0, rows // 2, transform, 0, unroll=2)
+    lax.fori_loop(0, rows // 2, transform, 0, unroll=8)
     at = 0
     for out in outs:
         count = out.shape[0]
@@ -103,25 +81,21 @@
 
 def channelize(sources, me, pfb_taps, one, twist_re, twist_im, two, tiles, counts):
     length = SECTION_ONE * SECTION_TWO
-
-    def index(at, skip, limit, i, me):
-        return (at, jnp.clip(i + skip, 0, limit), 0)
-
-    specs, operands = [], []
-    for held in sources:
-        for array, at, skip in held:
-            limit = array.shape[1] // FEED_TILE - 1
-            specs.append(
-                pl.BlockSpec((None, FEED_TILE, length), functools.partial(index, at, skip, limit))
-            )
-            operands.append(array)
+    specs = [
+        pl.BlockSpec(
+            (None, FEED_TILE, length),
+            functools.partial(lambda at, skip, i, me: (at, i + skip, 0), at, skip),
+        )
+        for _, at, skip in sources
+    ]
+    operands = [array for array, _, _ in sources]
     small = (pfb_taps, one, twist_re, twist_im)
     two_spec = pl.BlockSpec(
         (None,) + two.shape[1:], lambda i, me: (me[0], 0, 0), pipeline_mode=pl.Buffered(1)
     )
     feeds = tiles * FEED_TILE
     return pl.pallas_call(
-        functools.partial(channel_kernel, tuple(len(held) for held in sources)),
+        channel_kernel,
         grid_spec=pltpu.PrefetchScalarGridSpec(
             num_scalar_prefetch=1,
             grid=(tiles,),
@@ -153,7 +127,7 @@
 
 def block_of(voltages, at, first, feeds):
     length = voltages.shape[2]
-    rows = min(32, feeds)
+    rows = feeds // 2 if feeds > FEED_TILE else feeds
     skip = first // rows
     return pl.pallas_call(
         copy_kernel,
@@ -229,7 +203,7 @@
     )(*operands)
 
 
-def table_kernel(feeds, me, feed_of_slot, waves, out):
+def table_kernel(feeds, me, feed_of_slot, waves, out, found):
     rows = out.shape[0]
     slots = feed_of_slot.shape[0]
     lanes = waves.shape[1]
@@ -239,14 +213,20 @@
     m = row >> shift
     cosine = jnp.broadcast_to(waves[0:1, :], (rows, lanes))
     sine = jnp.broadcast_to(waves[1:2, :], (rows, lanes))
-    slot_index = lax.broadcasted_iota(jnp.int32, (slots, lanes), 0)
-    lane = lax.broadcasted_iota(jnp.int32, (1, lanes), 1)
+
+    @pl.when(pl.program_id(0) == 0)
+    def _():
+        slot_index = lax.broadcasted_iota(jnp.int32, (slots, lanes), 0)
+        lane = lax.broadcasted_iota(jnp.int32, (1, lanes), 1)
+        held = jnp.broadcast_to(feed_of_slot[...], (slots, lanes))
+        for at in range(0, slots, lanes):
+            place = at + lane
+            feed = ((place // feeds) ^ me[0]) * feeds + place % feeds
+            slot = jnp.sum(jnp.where(held == feed, slot_index, 0), axis=0, keepdims=True)
+            found[:, at : at + lanes] = jnp.broadcast_to(slot, (8, lanes))
+
     for at in range(0, slots, lanes):
-        place = at + lane
-        feed = ((place // feeds) ^ me[0]) * feeds + place % feeds
-        match = feed_of_slot[...] == feed
-        slot = jnp.sum(jnp.where(match, slot_index, 0), axis=0, keepdims=True)
-        slot = jnp.broadcast_to(slot, (rows, lanes))
+        slot = jnp.broadcast_to(found[0:1, at : at + lanes], (rows, lanes))
         cylinder = slot >> shift
         turn = p * (slot & (COL_FEEDS - 1)) + m * cylinder * (COL_FEEDS // CYLINDERS)
         turn = turn & (COL_FEEDS - 1)
@@ -275,6 +255,7 @@
             grid=(slots // rows,),
             in_specs=[whole_spec(column), whole_spec(waves)],
             out_specs=pl.BlockSpec((rows, 2 * slots), lambda i, me: (i, 0)),
+            scratch_shapes=[pltpu.VMEM((8, slots), jnp.int32)],
         ),
         out_shape=jax.ShapeDtypeStruct((slots, 2 * slots), BF16),
         compiler_params=pltpu.CompilerParams(
@@ -292,16 +273,10 @@
     times = lax.axis_size("tm")
     peers = lax.axis_size("feed")
     owned = KEPT // peers
-    half = feeds_here // 2
+    lead = max(1, 3 * feeds_here // (8 * FEED_TILE)) * FEED_TILE
     pairs = [(i + 1, i) for i in range(times - 1)]
-    halo = []
-    for i in range(spectra_here):
-        held = []
-        spans = [(0, half), (half, half)] if i == 0 else [(0, feeds_here)]
-        for first, count in spans:
-            block = block_of(voltages, i, first, count)
-            held.append((lax.ppermute(block, "tm", pairs), 0, -first // FEED_TILE))
-        halo.append(held)
+    early = lax.ppermute(block_of(voltages, 0, 0, lead), "tm", pairs)
+    following = lax.ppermute(voltages, "tm", pairs)
     me = lax.axis_index("feed").astype(jnp.int32).reshape(1)
     one = jnp.asarray(np.concatenate(tables(SECTION_ONE, SECTION_ONE, SECTION_ONE, 1.0))).astype(BF16)
     factor = 1.0 / math.sqrt(SECTION_ONE * SECTION_TWO)
@@ -315,22 +290,34 @@
         axis=1,
     ).reshape(peers, 2 * owned, 2 * SECTION_TWO)
     order = np.arange(peers)[:, None] ^ np.arange(peers)[None, :]
-    two = two[order].reshape(peers, 2 * KEPT, 2 * SECTION_TWO).astype(BF16)
+    two = two[order]
+
+    def split_table(shares):
+        held, at = [], 0
+        for wide in shares:
+            held.append(two[:, :, 2 * at : 2 * (at + wide)].reshape(peers, -1, 2 * SECTION_TWO))
+            at += wide
+        return jnp.asarray(np.concatenate(held, axis=1)).astype(BF16)
+
     table = beam_table(feed_of_slot, me, feeds_here)
+    first_spans = [(0, lead), (lead, feeds_here - lead)]
+    last_share = max(1, owned // 2)
     chunks = []
     for s in range(spectra_here):
-        spans = [(0, half), (half, half)] if s == 0 else [(0, feeds_here)]
-        gathered = [[] for _ in range(peers)]
-        for part, (first, count) in enumerate(spans):
+        spans = first_spans if s == 0 else [(0, feeds_here)]
+        shares = [owned - last_share, last_share] if s == spectra_here - 1 else [owned]
+        gathered = [[[] for _ in range(peers)] for _ in shares]
+        for first, count in spans:
+            skip = first // FEED_TILE
             sources = []
             for tap_index in range(pfb_taps.shape[0]):
                 at = s + tap_index
                 if at < spectra_here:
-                    sources.append([(voltages, at, first // FEED_TILE)])
-                elif s == 0:
-                    sources.append([(halo[0][part][0], 0, 0)])
+                    sources.append((voltages, at, skip))
+                elif s == 0 and first < lead:
+                    sources.append((early, 0, skip))
                 else:
-                    sources.append(halo[at - spectra_here])
+                    sources.append((following, at - spectra_here, skip))
             pieces = channelize(
                 sources,
                 me,
@@ -338,19 +325,22 @@
                 one,
                 twist_re,
                 twist_im,
-                two,
+                split_table(shares),
                 count // FEED_TILE,
-                [2 * owned] * peers,
+                [2 * wide for wide in shares for _ in range(peers)],
             )
-            gathered[0].append(pieces[0])
-            for j in reversed(range(1, peers)):
-                gathered[j].append(
-                    lax.ppermute(pieces[j], "feed", [(i, i ^ j) for i in range(peers)])
-                )
-        chunks.append(gathered)
+            for split in range(len(shares)):
+                mine = pieces[split * peers : (split + 1) * peers]
+                gathered[split][0].append(mine[0])
+                for j in reversed(range(1, peers)):
+                    gathered[split][j].append(
+                        lax.ppermute(mine[j], "feed", [(i, i ^ j) for i in range(peers)])
+                    )
+        for split, held in enumerate(gathered):
+            chunks.append((held, sum(shares[:split])))
     power = None
-    for arrived in chunks:
-        power = form_beams(arrived, table, power, owned * SECTION_ONE, 0)
+    for arrived, first in chunks:
+        power = form_beams(arrived, table, power, owned * SECTION_ONE, first)
     return power[None]
 
 

time: 438 us -> 377 us (0.86)
  Pallas kernels: 144 us -> 96 us
  starting transfers between devices: 63.4 us -> 55.1 us
    pallas_call x4, Pallas kernels: 81.6 us -> 49.4 us  [channelize(): pl.pallas_call(channel_kernel, grid_spec=pltpu.PrefetchScalarGridSpec(num...]
    pallas_call x4 -> x1, Pallas kernels: 14.9 us -> 2.37 us  [block_of(): pl.pallas_call(copy_kernel, grid=(feeds // rows,), in_specs=[pl.BlockSpec...]
    ppermute x32 -> x37, starting transfers between devices: 63.4 us -> 55.1 us  [the longest x35 50.7 us: on_device(): lax.ppermute(mine[j], 'feed', [(i, i ^ j) for i in range(peers)])]
    pallas_call x1, Pallas kernels: 13.1 us -> 6.71 us  [beam_table(): pl.pallas_call(functools.partial(table_kernel, feeds), grid_spec=pltpu.Pr...]
    pallas_call x3 -> x4, Pallas kernels: 34.9 us -> 37.5 us  [form_beams(): pl.pallas_call(functools.partial(beam_kernel, peers, parts, before is not...]
    ppermute x32 -> x37, waiting for transfers between devices: 223 us -> 223 us  [the longest x1 148 us: on_device(): early = lax.ppermute(block_of(voltages, 0, 0, lead), 'tm', pairs)]
  transfers between devices with their start and end apart: 32 -> 37, of which waited for: 14 -> 12; matrix products, arithmetic and copies ran while one was open for 0% -> 0% of each run, Pallas kernels for 29% -> 24%
where the time goes in v2:
time: 377 us
  waiting for transfers between devices  223 us (59%)
  Pallas kernels  96 us (25%)
  starting transfers between devices  55.1 us (15%)
    ppermute x1, waiting for transfers between devices, on_device(): early = lax.ppermute(block_of(voltages, 0, 0, lead), 'tm', pairs)  148 us
    ppermute x35, waiting for transfers between devices, on_device(): lax.ppermute(mine[j], 'feed', [(i, i ^ j) for i in range(peers)])  74.6 us
    ppermute x35, starting transfers between devices, on_device(): lax.ppermute(mine[j], 'feed', [(i, i ^ j) for i in range(peers)])  50.7 us
    pallas_call x4, Pallas kernels, channelize(): pl.pallas_call(channel_kernel, grid_spec=pltpu.PrefetchScalarGridSpec(num...  49.4 us
    pallas_call x4, Pallas kernels, form_beams(): pl.pallas_call(functools.partial(beam_kernel, peers, parts, before is not...  37.5 us
  transfers between devices with their start and end apart: 37, of which 12 were waited for; matrix products, arithmetic and copies ran while one was open for 0% of the time, Pallas kernels for 24%

profile of v2, /device:TPU:12, one launch (start us, length us, event | category | flops | bytes accessed | tf_op | source)
XLA Modules:
  0.0 376.5 jit_solution(5063683082230127605)
XLA Ops:
  0.0 1.9 collective-permute-start
  1.9 2.4 shard_map.112
  4.3 2.5 collective-permute-start.22
  6.8 148.2 %collective-permute-done.22.v3 = bf16[1,48,16384]{2,1,0:T(8,128)(2,1)} collective-permute-done((bf16[1,48,16384]{2,1,0:T(8,128)(2,1)}, bf16[1,48,16384]{2,1,0:T(8,128)(2,1)}, u32[]{:S(2)}, u32[]{:S(2)}) %collective-permute-start.22) | collective-permute-done | bytes 1572896 | tf_op jit(solution)/shard_map/ppermute | solution.py:278
  155.0 7.4 %shard_map.113 = (bf16[16,48,128]{2,1,0:T(8,128)(2,1)}, bf16[16,48,128]{2,1,0:T(8,128)(2,1)}, bf16[16,48,128]{2,1,0:T(8,128)(2,1)}, bf16[16,48,128]{2,1,0:T(8,12...) custom-call(s32[1]{0:T(128)} %bitcast.me, ...), custom_call_target="tpu_custom_call" | custom-call | flops 805306368 | bytes 7864320 | tf_op jit(solution)/shard_map/pallas_call | solution.py:97
  162.3 1.6 collective-permute-start.23
  163.9 0.5 collective-permute-start.25
  164.3 1.5 collective-permute-start.27
  165.9 2.6 collective-permute-start.29
  168.5 11.7 %collective-permute-done.23.refs_2_ = bf16[16,48,128]{2,1,0:T(8,128)(2,1)S(1)} collective-permute-done((bf16[16,48,128]{2,1,0:T(8,128)(2,1)}, bf16[16,48,128]{2,1,0:T(8,128)(2,1)S(1)}, u32[]{:S(2)}, u32[]{:S(2)}) %collective-permute-start.23) | collective-permute-done | bytes 196640 | tf_op jit(solution)/shard_map/ppermute | solution.py:337
  180.2 0.7 copy-done.6
  180.9 0.0 collective-permute-done.v1.v2.v3
  180.9 1.2 collective-permute-start.33
  182.0 15.8 %shard_map.109 = (bf16[8,128,128]{2,1,0:T(8,128)(2,1)}, bf16[8,128,128]{2,1,0:T(8,128)(2,1)}, bf16[8,128,128]{2,1,0:T(8,128)(2,1)}, bf16[8,128,128]{2,1,0:T(8,12...) custom-call(s32[1]{0:T(128)} %bitcast.me, ...), custom_call_target="tpu_custom_call" | custom-call | flops 2147483648 | bytes 20971520 | tf_op jit(solution)/shard_map/pallas_call | solution.py:97
  197.9 4.2 %collective-permute-start.10 = (bf16[8,128,128]{2,1,0:T(8,128)(2,1)}, bf16[8,128,128]{2,1,0:T(8,128)(2,1)}, u32[]{:S(2)}, u32[]{:S(2)}) collective-permute-start(bf16[8,128,128]{2,1,0:T(8,128)(2,1)} %get-tuple-element.56), channel_id=1, source_target_pairs={{0,3},{1,2},{2,1},{3,0},{4,7},{5,6},{6,5},{7,4},{8,11},{9,10},{10,... | collective-permute-start | bytes 786440 | tf_op jit(solution)/shard_map/ppermute | solution.py:337
  202.1 0.7 collective-permute-start.11
  202.7 0.0 collective-permute-done.29.refs_8_
  202.7 3.2 collective-permute-start.12
  205.9 0.0 collective-permute-done.31.refs_10_
  206.0 1.1 collective-permute-start.35
  207.1 10.7 %shard_map.114 = (bf16[16,80,128]{2,1,0:T(8,128)(2,1)}, bf16[16,80,128]{2,1,0:T(8,128)(2,1)}, bf16[16,80,128]{2,1,0:T(8,128)(2,1)}, bf16[16,80,128]{2,1,0:T(8,12...) custom-call(s32[1]{0:T(128)} %bitcast.me, ...), custom_call_target="tpu_custom_call" | custom-call | flops 1342177280 | bytes 13107200 | tf_op jit(solution)/shard_map/pallas_call | solution.py:97
  217.8 0.0 collective-permute-done.33.refs_12_
  217.8 1.5 collective-permute-start.24
  219.3 12.7 %collective-permute-done.35.refs_14_ = bf16[16,48,128]{2,1,0:T(8,128)(2,1)} collective-permute-done((bf16[16,48,128]{2,1,0:T(8,128)(2,1)}, bf16[16,48,128]{2,1,0:T(8,128)(2,1)}, u32[]{:S(2)}, u32[]{:S(2)}) %collective-permute-start.35) | collective-permute-done | bytes 196640 | tf_op jit(solution)/shard_map/ppermute | solution.py:337
  232.0 1.4 collective-permute-start.13
  233.4 0.0 collective-permute-done.10.refs_3_
  233.4 0.0 collective-permute-start.26
  233.4 2.2 collective-permute-start.28
  235.6 0.4 collective-permute-start.30
  236.0 15.4 %shard_map.111 = (bf16[16,128,128]{2,1,0:T(8,128)(2,1)}, bf16[16,128,128]{2,1,0:T(8,128)(2,1)}, bf16[16,128,128]{2,1,0:T(8,128)(2,1)}, bf16[16,128,128]{2,1,0:T(...) custom-call(s32[1]{0:T(128)} %bitcast.me, ...), custom_call_target="tpu_custom_call" | custom-call | flops 2147483648 | bytes 20971520 | tf_op jit(solution)/shard_map/pallas_call | solution.py:97
  251.5 1.1 collective-permute-start.15
  252.6 2.0 collective-permute-start.16
  254.5 1.1 collective-permute-start.32
  255.6 0.9 collective-permute-start.34
  256.5 1.8 collective-permute-start.36
  258.3 0.9 copy.15.feed_of_slot
  259.3 0.0 copy-start
  259.3 0.7 copy-done
  260.0 6.7 %shard_map.110.refs_16_.refs_8_ = bf16[1024,2048]{1,0:T(8,128)(2,1)S(1)} custom-call(s32[1]{0:T(128)} %bitcast.me, s32[1024,1]{1,0:T(8,128)S(1)} %copy.15.feed_of_slot, f32[8,128]{1,0:T(8,128)S(1)} %copy-done), custom_call_target="tpu_custom_call" | custom-call | flops 41943040 | bytes 4194304 | tf_op jit(solution)/shard_map/pallas_call | solution.py:251
  266.7 4.0 %collective-permute-start.17 = (bf16[16,128,128]{2,1,0:T(8,128)(2,1)S(1)}, bf16[16,128,128]{2,1,0:T(8,128)(2,1)S(1)}, u32[]{:S(2)}, u32[]{:S(2)}) collective-permute-start(bf16[16,128,128]{2,1,0:T(8,128)(2,1)S(1)} %copy-done.12), channel_id=1, source_target_pairs={{0,3},{1,2},{2,1},{3,0},{4,7},{5,6},{6,5},{7,4},{8,11},{9,10},{10,... | collective-permute-start | bytes 1572872 | tf_op jit(solution)/shard_map/ppermute | solution.py:337
  270.7 5.1 %collective-permute-done.34.refs_13_ = bf16[16,80,128]{2,1,0:T(8,128)(2,1)S(1)} collective-permute-done((bf16[16,80,128]{2,1,0:T(8,128)(2,1)}, bf16[16,80,128]{2,1,0:T(8,128)(2,1)S(1)}, u32[]{:S(2)}, u32[]{:S(2)}) %collective-permute-start.34) | collective-permute-done | bytes 327712 | tf_op jit(solution)/shard_map/ppermute | solution.py:337
  275.9 11.3 %collective-permute-done.36.refs_15_ = bf16[16,80,128]{2,1,0:T(8,128)(2,1)S(1)} collective-permute-done((bf16[16,80,128]{2,1,0:T(8,128)(2,1)}, bf16[16,80,128]{2,1,0:T(8,128)(2,1)S(1)}, u32[]{:S(2)}, u32[]{:S(2)}) %collective-permute-start.36) | collective-permute-done | bytes 327712 | tf_op jit(solution)/shard_map/ppermute | solution.py:337
  287.2 1.4 collective-permute-start.20
  288.6 1.2 collective-permute-start.21
  289.9 11.7 %shard_map.115.refs_9_ = f32[1024,1024]{1,0:T(8,128)} custom-call(bf16[16,48,128]{2,1,0:T(8,128)(2,1)S(1)} %copy-done.5, bf16[16,80,128]{2,1,0:T(8,128)(2,1)S(1)} %copy-done.2, bf16[16,48,128]{2,1,0:T(8,128)(2,1)S(1)} %copy-done.7, bf16[16,80,128]{2,1,0:T(8,128)(2,1)} %collective-permute-done.24.refs_3_, ...), custom_call_target="tpu_custom_call" | custom-call | flops 8589934592 | bytes 12582912 | tf_op jit(solution)/shard_map/pallas_call | solution.py:188
  301.6 1.8 collective-permute-start.14
  303.4 0.7 collective-permute-start.8
  304.2 12.1 %collective-permute-done.19.refs_5_ = bf16[16,128,128]{2,1,0:T(8,128)(2,1)S(1)} collective-permute-done((bf16[16,128,128]{2,1,0:T(8,128)(2,1)S(1)}, bf16[16,128,128]{2,1,0:T(8,128)(2,1)S(1)}, u32[]{:S(2)}, u32[]{:S(2)}) %collective-permute-start.19) | collective-permute-done | bytes 524320 | tf_op jit(solution)/shard_map/ppermute | solution.py:337
  316.2 3.4 collective-permute-start.9
  319.6 3.7 collective-permute-done.20.refs_6_
  323.3 0.9 collective-permute-start.1
  324.2 5.1 %collective-permute-done.21.refs_7_ = bf16[16,128,128]{2,1,0:T(8,128)(2,1)S(1)} collective-permute-done((bf16[16,128,128]{2,1,0:T(8,128)(2,1)S(1)}, bf16[16,128,128]{2,1,0:T(8,128)(2,1)S(1)}, u32[]{:S(2)}, u32[]{:S(2)}) %collective-permute-start.21) | collective-permute-done | bytes 524320 | tf_op jit(solution)/shard_map/ppermute | solution.py:337
  329.5 11.7 %shard_map.116.refs_9_ = f32[1024,1024]{1,0:T(8,128)} custom-call(bf16[16,128,128]{2,1,0:T(8,128)(2,1)S(1)} %copy-done.1, bf16[16,128,128]{2,1,0:T(8,128)(2,1)S(1)} %collective-permute-done.15.refs_1_, bf16[16,128,128]{2,1,0:T(8,128)(2,1)S(1)} %collective-permute-done.16.refs_2_, ...), custom_call_target="tpu_custom_call", output_to_operand_aliasing={{}: (9, {})} | custom-call | flops 8589934592 | bytes 12582912 | tf_op jit(solution)/shard_map/pallas_call | solution.py:188
  341.2 2.6 collective-permute-start.3
  343.8 0.5 collective-permute-start.4
  344.2 2.8 collective-permute-start.5
  347.1 1.4 collective-permute-start.6
  348.4 1.2 collective-permute-start.7
  349.7 7.2 %shard_map.117.refs_9_ = f32[1024,1024]{1,0:T(8,128)} custom-call(bf16[8,128,128]{2,1,0:T(8,128)(2,1)S(1)} %copy-done.4, bf16[8,128,128]{2,1,0:T(8,128)(2,1)S(1)} %collective-permute-done.8.refs_1_, bf16[8,128,128]{2,1,0:T(8,128)(2,1)S(1)} %collective-permute-done.9.refs_2_, ...), custom_call_target="tpu_custom_call", output_to_operand_aliasing={{}: (9, {})} | custom-call | flops 4294967296 | bytes 8388608 | tf_op jit(solution)/shard_map/pallas_call | solution.py:188
  356.9 2.5 collective-permute-done.4.refs_4_
  359.4 2.8 collective-permute-done.5.refs_5_
  362.2 4.3 %collective-permute-done.6.refs_6_ = bf16[8,128,128]{2,1,0:T(8,128)(2,1)S(1)} collective-permute-done((bf16[8,128,128]{2,1,0:T(8,128)(2,1)S(1)}, bf16[8,128,128]{2,1,0:T(8,128)(2,1)S(1)}, u32[]{:S(2)}, u32[]{:S(2)}) %collective-permute-start.6) | collective-permute-done | bytes 262176 | tf_op jit(solution)/shard_map/ppermute | solution.py:337
  366.5 3.2 collective-permute-done.7.refs_7_
  369.7 6.9 %shard_map.118 = f32[1024,1024]{1,0:T(8,128)} custom-call(bf16[8,128,128]{2,1,0:T(8,128)(2,1)S(1)} %copy-done.3, bf16[8,128,128]{2,1,0:T(8,128)(2,1)S(1)} %collective-permute-done.1.refs_1_, bf16[8,128,128]{2,1,0:T(8,128)(2,1)S(1)} %collective-permute-done.2.refs_2_, ...), custom_call_target="tpu_custom_call", output_to_operand_aliasing={{}: (9, {})} | custom-call | flops 4294967296 | bytes 8388608 | tf_op jit(solution)/shard_map/pallas_call | solution.py:188
  (67 shorter events, 0.1 us)
Async XLA Ops:
  0.0 180.9 %collective-permute-start = (bf16[3,128,16384]{2,1,0:T(8,128)(2,1)}, bf16[3,128,16384]{2,1,0:T(8,128)(2,1)}, u32[]{:S(2)}, u32[]{:S(2)}) collective-permute-start(bf16[3,128,16384]{2,1,0:T(8,128)(2,1)} %v2.3), channel_id=1, source_target_pairs={{8,0},{16,8},{24,16},{9,1},{17,9},{25,17},{10,2},{18,10},{26,18},{... | collective-permute-start | bytes 37748744 | tf_op jit(solution)/shard_map/ppermute | solution.py:279
  4.3 150.7 %collective-permute-start.22 = (bf16[1,48,16384]{2,1,0:T(8,128)(2,1)}, bf16[1,48,16384]{2,1,0:T(8,128)(2,1)}, u32[]{:S(2)}, u32[]{:S(2)}) collective-permute-start(bf16[1,48,16384]{2,1,0:T(8,128)(2,1)} %shard_map.112), channel_id=1, source_target_pairs={{8,0},{16,8},{24,16},{9,1},{17,9},{25,17},{10,2},{18,10},{26,18},{... | collective-permute-start | bytes 4718600 | tf_op jit(solution)/shard_map/ppermute | solution.py:278
  162.3 17.9 %collective-permute-start.23 = (bf16[16,48,128]{2,1,0:T(8,128)(2,1)}, bf16[16,48,128]{2,1,0:T(8,128)(2,1)S(1)}, u32[]{:S(2)}, u32[]{:S(2)}) collective-permute-start(bf16[16,48,128]{2,1,0:T(8,128)(2,1)} %get-tuple-element.71), channel_id=1, source_target_pairs={{0,1},{1,0},{2,3},{3,2},{4,5},{5,4},{6,7},{7,6},{8,9},{9,8},{10,11... | collective-permute-start | bytes 589832 | tf_op jit(solution)/shard_map/ppermute | solution.py:337
  163.9 34.0 %collective-permute-start.25 = (bf16[16,48,128]{2,1,0:T(8,128)(2,1)}, bf16[16,48,128]{2,1,0:T(8,128)(2,1)}, u32[]{:S(2)}, u32[]{:S(2)}) collective-permute-start(bf16[16,48,128]{2,1,0:T(8,128)(2,1)} %get-tuple-element.73), channel_id=1, source_target_pairs={{0,2},{1,3},{2,0},{3,1},{4,6},{5,7},{6,4},{7,5},{8,10},{9,11},{10,... | collective-permute-start | bytes 589832 | tf_op jit(solution)/shard_map/ppermute | solution.py:337
  164.3 37.7 %collective-permute-start.27 = (bf16[16,48,128]{2,1,0:T(8,128)(2,1)}, bf16[16,48,128]{2,1,0:T(8,128)(2,1)}, u32[]{:S(2)}, u32[]{:S(2)}) collective-permute-start(bf16[16,48,128]{2,1,0:T(8,128)(2,1)} %get-tuple-element.75), channel_id=1, source_target_pairs={{0,3},{1,2},{2,1},{3,0},{4,7},{5,6},{6,5},{7,4},{8,11},{9,10},{10,... | collective-permute-start | bytes 589832 | tf_op jit(solution)/shard_map/ppermute | solution.py:337
  165.9 36.9 %collective-permute-start.29 = (bf16[16,48,128]{2,1,0:T(8,128)(2,1)}, bf16[16,48,128]{2,1,0:T(8,128)(2,1)}, u32[]{:S(2)}, u32[]{:S(2)}) collective-permute-start(bf16[16,48,128]{2,1,0:T(8,128)(2,1)} %get-tuple-element.77), channel_id=1, source_target_pairs={{0,4},{1,5},{2,6},{3,7},{4,0},{5,1},{6,2},{7,3},{8,12},{9,13},{10,... | collective-permute-start | bytes 589832 | tf_op jit(solution)/shard_map/ppermute | solution.py:337
  180.2 0.7 copy-start.6
  180.9 25.1 %collective-permute-start.31 = (bf16[16,48,128]{2,1,0:T(8,128)(2,1)}, bf16[16,48,128]{2,1,0:T(8,128)(2,1)}, u32[]{:S(2)}, u32[]{:S(2)}) collective-permute-start(bf16[16,48,128]{2,1,0:T(8,128)(2,1)} %get-tuple-element.79), channel_id=1, source_target_pairs={{0,5},{1,4},{2,7},{3,6},{4,1},{5,0},{6,3},{7,2},{8,13},{9,12},{10,... | collective-permute-start | bytes 589832 | tf_op jit(solution)/shard_map/ppermute | solution.py:337
  180.9 36.9 %collective-permute-start.33 = (bf16[16,48,128]{2,1,0:T(8,128)(2,1)}, bf16[16,48,128]{2,1,0:T(8,128)(2,1)}, u32[]{:S(2)}, u32[]{:S(2)}) collective-permute-start(bf16[16,48,128]{2,1,0:T(8,128)(2,1)} %get-tuple-element.81), channel_id=1, source_target_pairs={{0,6},{1,7},{2,4},{3,5},{4,2},{5,3},{6,0},{7,1},{8,14},{9,15},{10,... | collective-permute-start | bytes 589832 | tf_op jit(solution)/shard_map/ppermute | solution.py:337
  197.9 35.5 %collective-permute-start.10 = (bf16[8,128,128]{2,1,0:T(8,128)(2,1)}, bf16[8,128,128]{2,1,0:T(8,128)(2,1)}, u32[]{:S(2)}, u32[]{:S(2)}) collective-permute-start(bf16[8,128,128]{2,1,0:T(8,128)(2,1)} %get-tuple-element.56), channel_id=1, source_target_pairs={{0,3},{1,2},{2,1},{3,0},{4,7},{5,6},{6,5},{7,4},{8,11},{9,10},{10,... | collective-permute-start | bytes 786440 | tf_op jit(solution)/shard_map/ppermute | solution.py:337
  202.1 31.3 %collective-permute-start.11 = (bf16[8,128,128]{2,1,0:T(8,128)(2,1)}, bf16[8,128,128]{2,1,0:T(8,128)(2,1)}, u32[]{:S(2)}, u32[]{:S(2)}) collective-permute-start(bf16[8,128,128]{2,1,0:T(8,128)(2,1)} %get-tuple-element.57), channel_id=1, source_target_pairs={{0,4},{1,5},{2,6},{3,7},{4,0},{5,1},{6,2},{7,3},{8,12},{9,13},{10,... | collective-permute-start | bytes 786440 | tf_op jit(solution)/shard_map/ppermute | solution.py:337
  202.7 32.8 %collective-permute-start.12 = (bf16[8,128,128]{2,1,0:T(8,128)(2,1)}, bf16[8,128,128]{2,1,0:T(8,128)(2,1)}, u32[]{:S(2)}, u32[]{:S(2)}) collective-permute-start(bf16[8,128,128]{2,1,0:T(8,128)(2,1)} %get-tuple-element.58), channel_id=1, source_target_pairs={{0,5},{1,4},{2,7},{3,6},{4,1},{5,0},{6,3},{7,2},{8,13},{9,12},{10,... | collective-permute-start | bytes 786440 | tf_op jit(solution)/shard_map/ppermute | solution.py:337
  206.0 26.0 %collective-permute-start.35 = (bf16[16,48,128]{2,1,0:T(8,128)(2,1)}, bf16[16,48,128]{2,1,0:T(8,128)(2,1)}, u32[]{:S(2)}, u32[]{:S(2)}) collective-permute-start(bf16[16,48,128]{2,1,0:T(8,128)(2,1)} %get-tuple-element.83), channel_id=1, source_target_pairs={{0,7},{1,6},{2,5},{3,4},{4,3},{5,2},{6,1},{7,0},{8,15},{9,14},{10,... | collective-permute-start | bytes 589832 | tf_op jit(solution)/shard_map/ppermute | solution.py:337
  217.8 34.8 %collective-permute-start.24 = (bf16[16,80,128]{2,1,0:T(8,128)(2,1)}, bf16[16,80,128]{2,1,0:T(8,128)(2,1)}, u32[]{:S(2)}, u32[]{:S(2)}) collective-permute-start(bf16[16,80,128]{2,1,0:T(8,128)(2,1)} %get-tuple-element.72), channel_id=1, source_target_pairs={{0,1},{1,0},{2,3},{3,2},{4,5},{5,4},{6,7},{7,6},{8,9},{9,8},{10,11... | collective-permute-start | bytes 983048 | tf_op jit(solution)/shard_map/ppermute | solution.py:337
  232.0 19.5 %collective-permute-start.13 = (bf16[8,128,128]{2,1,0:T(8,128)(2,1)}, bf16[8,128,128]{2,1,0:T(8,128)(2,1)}, u32[]{:S(2)}, u32[]{:S(2)}) collective-permute-start(bf16[8,128,128]{2,1,0:T(8,128)(2,1)} %get-tuple-element.59), channel_id=1, source_target_pairs={{0,6},{1,7},{2,4},{3,5},{4,2},{5,3},{6,0},{7,1},{8,14},{9,15},{10,... | collective-permute-start | bytes 786440 | tf_op jit(solution)/shard_map/ppermute | solution.py:337
  233.4 21.1 %collective-permute-start.26 = (bf16[16,80,128]{2,1,0:T(8,128)(2,1)}, bf16[16,80,128]{2,1,0:T(8,128)(2,1)}, u32[]{:S(2)}, u32[]{:S(2)}) collective-permute-start(bf16[16,80,128]{2,1,0:T(8,128)(2,1)} %get-tuple-element.74), channel_id=1, source_target_pairs={{0,2},{1,3},{2,0},{3,1},{4,6},{5,7},{6,4},{7,5},{8,10},{9,11},{10,... | collective-permute-start | bytes 983048 | tf_op jit(solution)/shard_map/ppermute | solution.py:337
  233.4 22.2 %collective-permute-start.28 = (bf16[16,80,128]{2,1,0:T(8,128)(2,1)}, bf16[16,80,128]{2,1,0:T(8,128)(2,1)}, u32[]{:S(2)}, u32[]{:S(2)}) collective-permute-start(bf16[16,80,128]{2,1,0:T(8,128)(2,1)} %get-tuple-element.76), channel_id=1, source_target_pairs={{0,3},{1,2},{2,1},{3,0},{4,7},{5,6},{6,5},{7,4},{8,11},{9,10},{10,... | collective-permute-start | bytes 983048 | tf_op jit(solution)/shard_map/ppermute | solution.py:337
  235.6 20.9 %collective-permute-start.30 = (bf16[16,80,128]{2,1,0:T(8,128)(2,1)}, bf16[16,80,128]{2,1,0:T(8,128)(2,1)}, u32[]{:S(2)}, u32[]{:S(2)}) collective-permute-start(bf16[16,80,128]{2,1,0:T(8,128)(2,1)} %get-tuple-element.78), channel_id=1, source_target_pairs={{0,4},{1,5},{2,6},{3,7},{4,0},{5,1},{6,2},{7,3},{8,12},{9,13},{10,... | collective-permute-start | bytes 983048 | tf_op jit(solution)/shard_map/ppermute | solution.py:337
  251.5 38.4 %copy-start.2 = (bf16[16,80,128]{2,1,0:T(8,128)(2,1)S(1)}, bf16[16,80,128]{2,1,0:T(8,128)(2,1)}, u32[]{:S(2)}) copy-start(bf16[16,80,128]{2,1,0:T(8,128)(2,1)} %get-tuple-element.70.refs_1_) | copy-start | bytes 983044
  251.5 38.4 %copy-start.5 = (bf16[16,48,128]{2,1,0:T(8,128)(2,1)S(1)}, bf16[16,48,128]{2,1,0:T(8,128)(2,1)}, u32[]{:S(2)}) copy-start(bf16[16,48,128]{2,1,0:T(8,128)(2,1)} %get-tuple-element.69.refs_0_) | copy-start | bytes 589828
  251.5 35.7 %collective-permute-start.15 = (bf16[16,128,128]{2,1,0:T(8,128)(2,1)}, bf16[16,128,128]{2,1,0:T(8,128)(2,1)S(1)}, u32[]{:S(2)}, u32[]{:S(2)}) collective-permute-start(bf16[16,128,128]{2,1,0:T(8,128)(2,1)} %get-tuple-element.62), channel_id=1, source_target_pairs={{0,1},{1,0},{2,3},{3,2},{4,5},{5,4},{6,7},{7,6},{8,9},{9,8},{10,11... | collective-permute-start | bytes 1572872 | tf_op jit(solution)/shard_map/ppermute | solution.py:337
  252.6 36.1 %collective-permute-start.16 = (bf16[16,128,128]{2,1,0:T(8,128)(2,1)}, bf16[16,128,128]{2,1,0:T(8,128)(2,1)S(1)}, u32[]{:S(2)}, u32[]{:S(2)}) collective-permute-start(bf16[16,128,128]{2,1,0:T(8,128)(2,1)} %get-tuple-element.63), channel_id=1, source_target_pairs={{0,2},{1,3},{2,0},{3,1},{4,6},{5,7},{6,4},{7,5},{8,10},{9,11},{10,... | collective-permute-start | bytes 1572872 | tf_op jit(solution)/shard_map/ppermute | solution.py:337
  254.5 12.2 %collective-permute-start.32 = (bf16[16,80,128]{2,1,0:T(8,128)(2,1)}, bf16[16,80,128]{2,1,0:T(8,128)(2,1)S(1)}, u32[]{:S(2)}, u32[]{:S(2)}) collective-permute-start(bf16[16,80,128]{2,1,0:T(8,128)(2,1)} %get-tuple-element.80), channel_id=1, source_target_pairs={{0,5},{1,4},{2,7},{3,6},{4,1},{5,0},{6,3},{7,2},{8,13},{9,12},{10,... | collective-permute-start | bytes 983048 | tf_op jit(solution)/shard_map/ppermute | solution.py:337
  255.6 20.3 %collective-permute-start.34 = (bf16[16,80,128]{2,1,0:T(8,128)(2,1)}, bf16[16,80,128]{2,1,0:T(8,128)(2,1)S(1)}, u32[]{:S(2)}, u32[]{:S(2)}) collective-permute-start(bf16[16,80,128]{2,1,0:T(8,128)(2,1)} %get-tuple-element.82), channel_id=1, source_target_pairs={{0,6},{1,7},{2,4},{3,5},{4,2},{5,3},{6,0},{7,1},{8,14},{9,15},{10,... | collective-permute-start | bytes 983048 | tf_op jit(solution)/shard_map/ppermute | solution.py:337
  256.5 30.6 %collective-permute-start.36 = (bf16[16,80,128]{2,1,0:T(8,128)(2,1)}, bf16[16,80,128]{2,1,0:T(8,128)(2,1)S(1)}, u32[]{:S(2)}, u32[]{:S(2)}) collective-permute-start(bf16[16,80,128]{2,1,0:T(8,128)(2,1)} %get-tuple-element.84), channel_id=1, source_target_pairs={{0,7},{1,6},{2,5},{3,4},{4,3},{5,2},{6,1},{7,0},{8,15},{9,14},{10,... | collective-permute-start | bytes 983048 | tf_op jit(solution)/shard_map/ppermute | solution.py:337
  259.3 0.7 copy-start
  259.9 6.8 %copy-start.12 = (bf16[16,128,128]{2,1,0:T(8,128)(2,1)S(1)}, bf16[16,128,128]{2,1,0:T(8,128)(2,1)}, u32[]{:S(2)}) copy-start(bf16[16,128,128]{2,1,0:T(8,128)(2,1)} %get-tuple-element.64) | copy-start | bytes 1572868
  259.9 15.9 %copy-start.11 = (bf16[16,128,128]{2,1,0:T(8,128)(2,1)S(1)}, bf16[16,128,128]{2,1,0:T(8,128)(2,1)}, u32[]{:S(2)}) copy-start(bf16[16,128,128]{2,1,0:T(8,128)(2,1)} %get-tuple-element.65) | copy-start | bytes 1572868
  260.0 27.2 %copy-start.10 = (bf16[16,128,128]{2,1,0:T(8,128)(2,1)S(1)}, bf16[16,128,128]{2,1,0:T(8,128)(2,1)}, u32[]{:S(2)}) copy-start(bf16[16,128,128]{2,1,0:T(8,128)(2,1)} %get-tuple-element.66) | copy-start | bytes 1572868
  260.0 27.2 %copy-start.9 = (bf16[16,128,128]{2,1,0:T(8,128)(2,1)S(1)}, bf16[16,128,128]{2,1,0:T(8,128)(2,1)}, u32[]{:S(2)}) copy-start(bf16[16,128,128]{2,1,0:T(8,128)(2,1)} %get-tuple-element.67) | copy-start | bytes 1572868
  260.0 28.7 %copy-start.8 = (bf16[16,128,128]{2,1,0:T(8,128)(2,1)S(1)}, bf16[16,128,128]{2,1,0:T(8,128)(2,1)}, u32[]{:S(2)}) copy-start(bf16[16,128,128]{2,1,0:T(8,128)(2,1)} %get-tuple-element.68) | copy-start | bytes 1572868
  260.0 29.9 %copy-start.7 = (bf16[16,48,128]{2,1,0:T(8,128)(2,1)S(1)}, bf16[16,48,128]{2,1,0:T(8,128)(2,1)}, u32[]{:S(2)}) copy-start(bf16[16,48,128]{2,1,0:T(8,128)(2,1)} %copy-done.6) | copy-start | bytes 589828
  266.7 34.9 %collective-permute-start.17 = (bf16[16,128,128]{2,1,0:T(8,128)(2,1)S(1)}, bf16[16,128,128]{2,1,0:T(8,128)(2,1)S(1)}, u32[]{:S(2)}, u32[]{:S(2)}) collective-permute-start(bf16[16,128,128]{2,1,0:T(8,128)(2,1)S(1)} %copy-done.12), channel_id=1, source_target_pairs={{0,3},{1,2},{2,1},{3,0},{4,7},{5,6},{6,5},{7,4},{8,11},{9,10},{10,... | collective-permute-start | bytes 1572872 | tf_op jit(solution)/shard_map/ppermute | solution.py:337
  275.9 27.6 %collective-permute-start.18 = (bf16[16,128,128]{2,1,0:T(8,128)(2,1)S(1)}, bf16[16,128,128]{2,1,0:T(8,128)(2,1)S(1)}, u32[]{:S(2)}, u32[]{:S(2)}) collective-permute-start(bf16[16,128,128]{2,1,0:T(8,128)(2,1)S(1)} %copy-done.11), channel_id=1, source_target_pairs={{0,4},{1,5},{2,6},{3,7},{4,0},{5,1},{6,2},{7,3},{8,12},{9,13},{10,... | collective-permute-start | bytes 1572872 | tf_op jit(solution)/shard_map/ppermute | solution.py:337
  287.2 29.1 %collective-permute-start.19 = (bf16[16,128,128]{2,1,0:T(8,128)(2,1)S(1)}, bf16[16,128,128]{2,1,0:T(8,128)(2,1)S(1)}, u32[]{:S(2)}, u32[]{:S(2)}) collective-permute-start(bf16[16,128,128]{2,1,0:T(8,128)(2,1)S(1)} %copy-done.10), channel_id=1, source_target_pairs={{0,5},{1,4},{2,7},{3,6},{4,1},{5,0},{6,3},{7,2},{8,13},{9,12},{10,... | collective-permute-start | bytes 1572872 | tf_op jit(solution)/shard_map/ppermute | solution.py:337
  287.2 36.1 %collective-permute-start.20 = (bf16[16,128,128]{2,1,0:T(8,128)(2,1)S(1)}, bf16[16,128,128]{2,1,0:T(8,128)(2,1)S(1)}, u32[]{:S(2)}, u32[]{:S(2)}) collective-permute-start(bf16[16,128,128]{2,1,0:T(8,128)(2,1)S(1)} %copy-done.9), channel_id=1, source_target_pairs={{0,6},{1,7},{2,4},{3,5},{4,2},{5,3},{6,0},{7,1},{8,14},{9,15},{10,... | collective-permute-start | bytes 1572872 | tf_op jit(solution)/shard_map/ppermute | solution.py:337
  288.6 40.8 %collective-permute-start.21 = (bf16[16,128,128]{2,1,0:T(8,128)(2,1)S(1)}, bf16[16,128,128]{2,1,0:T(8,128)(2,1)S(1)}, u32[]{:S(2)}, u32[]{:S(2)}) collective-permute-start(bf16[16,128,128]{2,1,0:T(8,128)(2,1)S(1)} %copy-done.8), channel_id=1, source_target_pairs={{0,7},{1,6},{2,5},{3,4},{4,3},{5,2},{6,1},{7,0},{8,15},{9,14},{10,... | collective-permute-start | bytes 1572872 | tf_op jit(solution)/shard_map/ppermute | solution.py:337
  289.8 11.8 %copy-start.22 = (bf16[8,128,128]{2,1,0:T(8,128)(2,1)S(1)}, bf16[8,128,128]{2,1,0:T(8,128)(2,1)}, u32[]{:S(2)}) copy-start(bf16[8,128,128]{2,1,0:T(8,128)(2,1)} %get-tuple-element.60) | copy-start | bytes 786436
  289.9 13.6 %copy-start.21 = (bf16[8,128,128]{2,1,0:T(8,128)(2,1)S(1)}, bf16[8,128,128]{2,1,0:T(8,128)(2,1)}, u32[]{:S(2)}) copy-start(bf16[8,128,128]{2,1,0:T(8,128)(2,1)} %get-tuple-element.54) | copy-start | bytes 786436
  289.9 26.4 %copy-start.20 = (bf16[8,128,128]{2,1,0:T(8,128)(2,1)S(1)}, bf16[8,128,128]{2,1,0:T(8,128)(2,1)}, u32[]{:S(2)}) copy-start(bf16[8,128,128]{2,1,0:T(8,128)(2,1)} %get-tuple-element.55) | copy-start | bytes 786436
  289.9 33.5 %copy-start.19 = (bf16[8,128,128]{2,1,0:T(8,128)(2,1)S(1)}, bf16[8,128,128]{2,1,0:T(8,128)(2,1)}, u32[]{:S(2)}) copy-start(bf16[8,128,128]{2,1,0:T(8,128)(2,1)} %get-tuple-element.46) | copy-start | bytes 786436
  289.9 39.5 %copy-start.18 = (bf16[8,128,128]{2,1,0:T(8,128)(2,1)S(1)}, bf16[8,128,128]{2,1,0:T(8,128)(2,1)}, u32[]{:S(2)}) copy-start(bf16[8,128,128]{2,1,0:T(8,128)(2,1)} %get-tuple-element.47) | copy-start | bytes 786436
  289.9 39.5 %copy-start.1 = (bf16[16,128,128]{2,1,0:T(8,128)(2,1)S(1)}, bf16[16,128,128]{2,1,0:T(8,128)(2,1)}, u32[]{:S(2)}) copy-start(bf16[16,128,128]{2,1,0:T(8,128)(2,1)} %get-tuple-element.61.refs_0_) | copy-start | bytes 1572868
  301.6 39.6 %collective-permute-start.14 = (bf16[8,128,128]{2,1,0:T(8,128)(2,1)S(1)}, bf16[8,128,128]{2,1,0:T(8,128)(2,1)S(1)}, u32[]{:S(2)}, u32[]{:S(2)}) collective-permute-start(bf16[8,128,128]{2,1,0:T(8,128)(2,1)S(1)} %copy-done.22), channel_id=1, source_target_pairs={{0,7},{1,6},{2,5},{3,4},{4,3},{5,2},{6,1},{7,0},{8,15},{9,14},{10,... | collective-permute-start | bytes 786440 | tf_op jit(solution)/shard_map/ppermute | solution.py:337
  303.4 40.4 %collective-permute-start.8 = (bf16[8,128,128]{2,1,0:T(8,128)(2,1)S(1)}, bf16[8,128,128]{2,1,0:T(8,128)(2,1)S(1)}, u32[]{:S(2)}, u32[]{:S(2)}) collective-permute-start(bf16[8,128,128]{2,1,0:T(8,128)(2,1)S(1)} %copy-done.21), channel_id=1, source_target_pairs={{0,1},{1,0},{2,3},{3,2},{4,5},{5,4},{6,7},{7,6},{8,9},{9,8},{10,11... | collective-permute-start | bytes 786440 | tf_op jit(solution)/shard_map/ppermute | solution.py:337
  316.2 28.0 %collective-permute-start.9 = (bf16[8,128,128]{2,1,0:T(8,128)(2,1)S(1)}, bf16[8,128,128]{2,1,0:T(8,128)(2,1)S(1)}, u32[]{:S(2)}, u32[]{:S(2)}) collective-permute-start(bf16[8,128,128]{2,1,0:T(8,128)(2,1)S(1)} %copy-done.20), channel_id=1, source_target_pairs={{0,2},{1,3},{2,0},{3,1},{4,6},{5,7},{6,4},{7,5},{8,10},{9,11},{10,... | collective-permute-start | bytes 786440 | tf_op jit(solution)/shard_map/ppermute | solution.py:337
  323.3 23.7 %collective-permute-start.1 = (bf16[8,128,128]{2,1,0:T(8,128)(2,1)S(1)}, bf16[8,128,128]{2,1,0:T(8,128)(2,1)S(1)}, u32[]{:S(2)}, u32[]{:S(2)}) collective-permute-start(bf16[8,128,128]{2,1,0:T(8,128)(2,1)S(1)} %copy-done.19), channel_id=1, source_target_pairs={{0,1},{1,0},{2,3},{3,2},{4,5},{5,4},{6,7},{7,6},{8,9},{9,8},{10,11... | collective-permute-start | bytes 786440 | tf_op jit(solution)/shard_map/ppermute | solution.py:337
  329.4 19.0 %collective-permute-start.2 = (bf16[8,128,128]{2,1,0:T(8,128)(2,1)S(1)}, bf16[8,128,128]{2,1,0:T(8,128)(2,1)S(1)}, u32[]{:S(2)}, u32[]{:S(2)}) collective-permute-start(bf16[8,128,128]{2,1,0:T(8,128)(2,1)S(1)} %copy-done.18), channel_id=1, source_target_pairs={{0,2},{1,3},{2,0},{3,1},{4,6},{5,7},{6,4},{7,5},{8,10},{9,11},{10,... | collective-permute-start | bytes 786440 | tf_op jit(solution)/shard_map/ppermute | solution.py:337
  329.4 11.8 %copy-start.17 = (bf16[8,128,128]{2,1,0:T(8,128)(2,1)S(1)}, bf16[8,128,128]{2,1,0:T(8,128)(2,1)}, u32[]{:S(2)}) copy-start(bf16[8,128,128]{2,1,0:T(8,128)(2,1)} %get-tuple-element.48) | copy-start | bytes 786436
  329.4 14.4 %copy-start.16 = (bf16[8,128,128]{2,1,0:T(8,128)(2,1)S(1)}, bf16[8,128,128]{2,1,0:T(8,128)(2,1)}, u32[]{:S(2)}) copy-start(bf16[8,128,128]{2,1,0:T(8,128)(2,1)} %get-tuple-element.49) | copy-start | bytes 786436
  329.4 14.8 %copy-start.15 = (bf16[8,128,128]{2,1,0:T(8,128)(2,1)S(1)}, bf16[8,128,128]{2,1,0:T(8,128)(2,1)}, u32[]{:S(2)}) copy-start(bf16[8,128,128]{2,1,0:T(8,128)(2,1)} %get-tuple-element.50) | copy-start | bytes 786436
  329.4 17.6 %copy-start.14 = (bf16[8,128,128]{2,1,0:T(8,128)(2,1)S(1)}, bf16[8,128,128]{2,1,0:T(8,128)(2,1)}, u32[]{:S(2)}) copy-start(bf16[8,128,128]{2,1,0:T(8,128)(2,1)} %get-tuple-element.51) | copy-start | bytes 786436
  329.4 19.0 %copy-start.13 = (bf16[8,128,128]{2,1,0:T(8,128)(2,1)S(1)}, bf16[8,128,128]{2,1,0:T(8,128)(2,1)}, u32[]{:S(2)}) copy-start(bf16[8,128,128]{2,1,0:T(8,128)(2,1)} %get-tuple-element.52) | copy-start | bytes 786436
  329.5 20.2 %copy-start.4 = (bf16[8,128,128]{2,1,0:T(8,128)(2,1)S(1)}, bf16[8,128,128]{2,1,0:T(8,128)(2,1)}, u32[]{:S(2)}) copy-start(bf16[8,128,128]{2,1,0:T(8,128)(2,1)} %get-tuple-element.53.refs_0_) | copy-start | bytes 786436
  341.2 15.7 %collective-permute-start.3 = (bf16[8,128,128]{2,1,0:T(8,128)(2,1)S(1)}, bf16[8,128,128]{2,1,0:T(8,128)(2,1)S(1)}, u32[]{:S(2)}, u32[]{:S(2)}) collective-permute-start(bf16[8,128,128]{2,1,0:T(8,128)(2,1)S(1)} %copy-done.17), channel_id=1, source_target_pairs={{0,3},{1,2},{2,1},{3,0},{4,7},{5,6},{6,5},{7,4},{8,11},{9,10},{10,... | collective-permute-start | bytes 786440 | tf_op jit(solution)/shard_map/ppermute | solution.py:337
  343.8 15.6 %collective-permute-start.4 = (bf16[8,128,128]{2,1,0:T(8,128)(2,1)S(1)}, bf16[8,128,128]{2,1,0:T(8,128)(2,1)S(1)}, u32[]{:S(2)}, u32[]{:S(2)}) collective-permute-start(bf16[8,128,128]{2,1,0:T(8,128)(2,1)S(1)} %copy-done.16), channel_id=1, source_target_pairs={{0,4},{1,5},{2,6},{3,7},{4,0},{5,1},{6,2},{7,3},{8,12},{9,13},{10,... | collective-permute-start | bytes 786440 | tf_op jit(solution)/shard_map/ppermute | solution.py:337
  344.2 18.0 %collective-permute-start.5 = (bf16[8,128,128]{2,1,0:T(8,128)(2,1)S(1)}, bf16[8,128,128]{2,1,0:T(8,128)(2,1)S(1)}, u32[]{:S(2)}, u32[]{:S(2)}) collective-permute-start(bf16[8,128,128]{2,1,0:T(8,128)(2,1)S(1)} %copy-done.15), channel_id=1, source_target_pairs={{0,5},{1,4},{2,7},{3,6},{4,1},{5,0},{6,3},{7,2},{8,13},{9,12},{10,... | collective-permute-start | bytes 786440 | tf_op jit(solution)/shard_map/ppermute | solution.py:337
  347.1 19.4 %collective-permute-start.6 = (bf16[8,128,128]{2,1,0:T(8,128)(2,1)S(1)}, bf16[8,128,128]{2,1,0:T(8,128)(2,1)S(1)}, u32[]{:S(2)}, u32[]{:S(2)}) collective-permute-start(bf16[8,128,128]{2,1,0:T(8,128)(2,1)S(1)} %copy-done.14), channel_id=1, source_target_pairs={{0,6},{1,7},{2,4},{3,5},{4,2},{5,3},{6,0},{7,1},{8,14},{9,15},{10,... | collective-permute-start | bytes 786440 | tf_op jit(solution)/shard_map/ppermute | solution.py:337
  348.4 21.2 %collective-permute-start.7 = (bf16[8,128,128]{2,1,0:T(8,128)(2,1)S(1)}, bf16[8,128,128]{2,1,0:T(8,128)(2,1)S(1)}, u32[]{:S(2)}, u32[]{:S(2)}) collective-permute-start(bf16[8,128,128]{2,1,0:T(8,128)(2,1)S(1)} %copy-done.13), channel_id=1, source_target_pairs={{0,7},{1,6},{2,5},{3,4},{4,3},{5,2},{6,1},{7,0},{8,15},{9,14},{10,... | collective-permute-start | bytes 786440 | tf_op jit(solution)/shard_map/ppermute | solution.py:337
  349.6 20.0 %copy-start.3 = (bf16[8,128,128]{2,1,0:T(8,128)(2,1)S(1)}, bf16[8,128,128]{2,1,0:T(8,128)(2,1)}, u32[]{:S(2)}) copy-start(bf16[8,128,128]{2,1,0:T(8,128)(2,1)} %get-tuple-element.45.refs_0_) | copy-start | bytes 786436

commit v3 on v2

--- a/solution.py
+++ b/solution.py
@@ -148,28 +148,54 @@
     count = peers * parts
     arrived, table, out = refs[:count], refs[count], refs[-1]
     before = refs[count + 1] if has_before else None
-    slots, lanes = table.shape[0], arrived[0].shape[2]
+    lanes = arrived[0].shape[2]
+    half, rows = COL_FEEDS // 2, COL_FEEDS // 2 + 8
+    line = lax.broadcasted_iota(jnp.int32, (8, lanes), 0)
+    mirror = (8 - line) & 7
     for i in range(arrived[0].shape[0] // 2):
-        real = jnp.concatenate([a[2 * i] for a in arrived], axis=0)
-        imag = jnp.concatenate([a[2 * i + 1] for a in arrived], axis=0)
         data = jnp.concatenate(
-            [jnp.concatenate([real, imag], axis=1), jnp.concatenate([-imag, real], axis=1)],
-            axis=0,
+            [
+                jnp.concatenate([a[2 * i + e] for a in arrived], axis=0)
+                for e in range(2)
+            ],
+            axis=1,
         )
         at = slice(i * lanes, (i + 1) * lanes)
-        step = 512
-        for row in range(0, slots, step):
-            beam = jnp.dot(table[row : row + step, :], data, preferred_element_type=F32)
-            power = beam[:, :lanes] * beam[:, :lanes] + beam[:, lanes:] * beam[:, lanes:]
+
+        def put(first, power):
+            to = slice(first, first + half)
             if before is not None:
-                power = power + before[row : row + step, at]
-            out[row : row + step, at] = power
+                power = power + before[to, at]
+            out[to, at] = power
+
+        for m in range(CYLINDERS):
+            both = jnp.dot(
+                table[2 * m * rows : 2 * (m + 1) * rows, :], data, preferred_element_type=F32
+            )
+            cos_re, cos_im = both[:rows, :lanes], both[:rows, lanes:]
+            sin_re, sin_im = both[rows:, :lanes], both[rows:, lanes:]
+            real = cos_re[:half] - sin_im[:half]
+            imag = cos_im[:half] + sin_re[:half]
+            put(m * COL_FEEDS, real * real + imag * imag)
+            real = cos_re + sin_im
+            imag = cos_im - sin_re
+            power = real * real + imag * imag
+            tiles = [
+                jnp.take_along_axis(power[8 * k : 8 * k + 8], mirror, axis=0)
+                for k in range(rows // 8)
+            ]
+            turned = [
+                jnp.where(line == 0, tiles[half // 8 - t], tiles[half // 8 - 1 - t])
+                for t in range(half // 8)
+            ]
+            other = (CYLINDERS - m) % CYLINDERS
+            put(other * COL_FEEDS + half, jnp.concatenate(turned, axis=0))
 
 
 def form_beams(arrived, table, before, channels, first):
     peers, parts = len(arrived), len(arrived[0])
     rows, _, lanes = arrived[0][0].shape
-    slots = table.shape[0]
+    slots = table.shape[1]
     width = min(2, rows // 2)
     offset = first // width
     out_spec = pl.BlockSpec((slots, width * lanes), lambda i: (0, i + offset))
@@ -196,7 +222,7 @@
             dimension_semantics=("arbitrary",), vmem_limit_bytes=24 << 20
         ),
         cost_estimate=pl.CostEstimate(
-            flops=8 * slots * slots * steps * width * lanes,
+            flops=4 * slots * slots * steps * width * lanes,
             bytes_accessed=8 * slots * steps * width * lanes + 4 * slots * slots,
             transcendentals=0,
         ),
@@ -208,11 +234,12 @@
     slots = feed_of_slot.shape[0]
     lanes = waves.shape[1]
     shift = COL_FEEDS.bit_length() - 1
-    row = pl.program_id(0) * rows + lax.broadcasted_iota(jnp.int32, (rows, lanes), 0)
-    p = row & (COL_FEEDS - 1)
-    m = row >> shift
+    row = lax.broadcasted_iota(jnp.int32, (rows, lanes), 0)
+    m = pl.program_id(0)
+    lower = row >= rows // 2
+    p = jnp.where(lower, row - rows // 2, row)
+    quarter = jnp.where(lower, COL_FEEDS // 4, 0)
     cosine = jnp.broadcast_to(waves[0:1, :], (rows, lanes))
-    sine = jnp.broadcast_to(waves[1:2, :], (rows, lanes))
 
     @pl.when(pl.program_id(0) == 0)
     def _():
@@ -229,13 +256,9 @@
         slot = jnp.broadcast_to(found[0:1, at : at + lanes], (rows, lanes))
         cylinder = slot >> shift
         turn = p * (slot & (COL_FEEDS - 1)) + m * cylinder * (COL_FEEDS // CYLINDERS)
-        turn = turn & (COL_FEEDS - 1)
-        index = turn & (lanes - 1)
-        real = jnp.take_along_axis(cosine, index, axis=1)
-        imag = jnp.take_along_axis(sine, index, axis=1)
-        flip = turn >= lanes
-        out[:, at : at + lanes] = jnp.where(flip, -real, real).astype(BF16)
-        out[:, slots + at : slots + at + lanes] = jnp.where(flip, -imag, imag).astype(BF16)
+        turn = (turn + quarter) & (COL_FEEDS - 1)
+        value = jnp.take_along_axis(cosine, turn & (lanes - 1), axis=1)
+        out[:, at : at + lanes] = jnp.where(turn >= lanes, -value, value).astype(BF16)
 
 
 def beam_table(feed_of_slot, me, feeds):
@@ -245,19 +268,18 @@
     angles = np.arange(half) * (2.0 * math.pi / COL_FEEDS)
     waves = np.zeros((8, half), np.float32)
     waves[0] = np.cos(angles) * factor
-    waves[1] = -np.sin(angles) * factor
-    rows = 256
+    rows = 2 * (half + 8)
     column = feed_of_slot.reshape(slots, 1)
     return pl.pallas_call(
         functools.partial(table_kernel, feeds),
         grid_spec=pltpu.PrefetchScalarGridSpec(
             num_scalar_prefetch=1,
-            grid=(slots // rows,),
+            grid=(CYLINDERS,),
             in_specs=[whole_spec(column), whole_spec(waves)],
-            out_specs=pl.BlockSpec((rows, 2 * slots), lambda i, me: (i, 0)),
+            out_specs=pl.BlockSpec((rows, slots), lambda i, me: (i, 0)),
             scratch_shapes=[pltpu.VMEM((8, slots), jnp.int32)],
         ),
-        out_shape=jax.ShapeDtypeStruct((slots, 2 * slots), BF16),
+        out_shape=jax.ShapeDtypeStruct((CYLINDERS * rows, slots), BF16),
         compiler_params=pltpu.CompilerParams(
             dimension_semantics=("arbitrary",), vmem_limit_bytes=24 << 20
         ),
@@ -273,7 +295,7 @@
     times = lax.axis_size("tm")
     peers = lax.axis_size("feed")
     owned = KEPT // peers
-    lead = max(1, 3 * feeds_here // (8 * FEED_TILE)) * FEED_TILE
+    lead = max(1, feeds_here // (4 * FEED_TILE)) * FEED_TILE
     pairs = [(i + 1, i) for i in range(times - 1)]
     early = lax.ppermute(block_of(voltages, 0, 0, lead), "tm", pairs)
     following = lax.ppermute(voltages, "tm", pairs)

time: 377 us -> 382 us (1.013)
  the two profiles are of different devices: /device:TPU:12 before, /device:TPU:11 now
where the time goes in v3:
time: 382 us; the launch traced here: 381 us
  waiting for transfers between devices  244 us (64%)
  Pallas kernels  82.4 us (22%)
  starting transfers between devices  41.8 us (11%)
  local copies, waits for them, and re-layouts  12.3 us (3%)
    ppermute x1, waiting for transfers between devices, on_device(): early = lax.ppermute(block_of(voltages, 0, 0, lead), 'tm', pairs)  145 us
    ppermute x35, waiting for transfers between devices, on_device(): lax.ppermute(mine[j], 'feed', [(i, i ^ j) for i in range(peers)])  99.4 us
    pallas_call x4, Pallas kernels, channelize(): pl.pallas_call(channel_kernel, grid_spec=pltpu.PrefetchScalarGridSpec(num...  49.4 us
    ppermute x35, starting transfers between devices, on_device(): lax.ppermute(mine[j], 'feed', [(i, i ^ j) for i in range(peers)])  37.3 us
    pallas_call x4, Pallas kernels, form_beams(): pl.pallas_call(functools.partial(beam_kernel, peers, parts, before is not...  27.1 us
    unnamed x50, local copies, waits for them, and re-layouts  11.4 us
  transfers between devices with their start and end apart: 37, of which 11 were waited for; matrix products, arithmetic and copies ran while one was open for 0% of the time, Pallas kernels for 20%

profile of v3, /device:TPU:11, one launch (start us, length us, event | category | flops | bytes accessed | tf_op | source)
XLA Modules:
  0.0 381.1 jit_solution(14180374895171695568)
XLA Ops:
  0.0 2.6 collective-permute-start
  2.6 2.1 shard_map.112
  4.6 1.9 collective-permute-start.22
  6.6 144.9 %collective-permute-done.22.v3 = bf16[1,32,16384]{2,1,0:T(8,128)(2,1)} collective-permute-done((bf16[1,32,16384]{2,1,0:T(8,128)(2,1)}, bf16[1,32,16384]{2,1,0:T(8,128)(2,1)}, u32[]{:S(2)}, u32[]{:S(2)}) %collective-permute-start.22) | collective-permute-done | bytes 1048608 | tf_op jit(solution)/shard_map/ppermute | solution.py:300
  151.5 5.8 %shard_map.113 = (bf16[16,32,128]{2,1,0:T(8,128)(2,1)}, bf16[16,32,128]{2,1,0:T(8,128)(2,1)}, bf16[16,32,128]{2,1,0:T(8,128)(2,1)}, bf16[16,32,128]{2,1,0:T(8,12...) custom-call(s32[1]{0:T(128)} %bitcast.me, ...), custom_call_target="tpu_custom_call" | custom-call | flops 536870912 | bytes 5242880 | tf_op jit(solution)/shard_map/pallas_call | solution.py:97
  157.3 0.3 collective-permute-start.23
  157.7 0.2 collective-permute-start.25
  157.8 2.2 collective-permute-start.27
  160.1 2.3 collective-permute-start.29
  162.4 15.8 %shard_map.109 = (bf16[8,128,128]{2,1,0:T(8,128)(2,1)}, bf16[8,128,128]{2,1,0:T(8,128)(2,1)}, bf16[8,128,128]{2,1,0:T(8,128)(2,1)}, bf16[8,128,128]{2,1,0:T(8,12...) custom-call(s32[1]{0:T(128)} %bitcast.me, ...), custom_call_target="tpu_custom_call" | custom-call | flops 2147483648 | bytes 20971520 | tf_op jit(solution)/shard_map/pallas_call | solution.py:97
  178.2 1.2 collective-permute-start.10
  179.4 2.3 collective-permute-start.11
  181.7 0.0 collective-permute-start.12
  181.8 3.8 collective-permute-done.29.refs_8_
  185.5 4.9 %collective-permute-done.31.refs_10_ = bf16[16,32,128]{2,1,0:T(8,128)(2,1)} collective-permute-done((bf16[16,32,128]{2,1,0:T(8,128)(2,1)}, bf16[16,32,128]{2,1,0:T(8,128)(2,1)}, u32[]{:S(2)}, u32[]{:S(2)}) %collective-permute-start.31) | collective-permute-done | bytes 131104 | tf_op jit(solution)/shard_map/ppermute | solution.py:359
  190.4 29.8 %collective-permute-done.33.refs_12_ = bf16[16,32,128]{2,1,0:T(8,128)(2,1)S(1)} collective-permute-done((bf16[16,32,128]{2,1,0:T(8,128)(2,1)}, bf16[16,32,128]{2,1,0:T(8,128)(2,1)S(1)}, u32[]{:S(2)}, u32[]{:S(2)}) %collective-permute-start.33) | collective-permute-done | bytes 131104 | tf_op jit(solution)/shard_map/ppermute | solution.py:359
  220.2 0.7 copy-done.16
  220.8 1.4 collective-permute-start.13
  222.3 10.0 %collective-permute-done.35.refs_14_ = bf16[16,32,128]{2,1,0:T(8,128)(2,1)S(1)} collective-permute-done((bf16[16,32,128]{2,1,0:T(8,128)(2,1)}, bf16[16,32,128]{2,1,0:T(8,128)(2,1)S(1)}, u32[]{:S(2)}, u32[]{:S(2)}) %collective-permute-start.35) | collective-permute-done | bytes 131104 | tf_op jit(solution)/shard_map/ppermute | solution.py:359
  232.2 0.7 copy-done.18
  232.9 1.1 collective-permute-start.14
  234.0 0.7 copy-done.2
  234.7 1.3 collective-permute-start.8
  236.0 0.7 copy-done.4
  236.7 0.7 copy-done.6
  237.5 0.2 collective-permute-start.1
  237.6 12.3 %shard_map.114 = (bf16[16,96,128]{2,1,0:T(8,128)(2,1)}, bf16[16,96,128]{2,1,0:T(8,128)(2,1)}, bf16[16,96,128]{2,1,0:T(8,128)(2,1)}, bf16[16,96,128]{2,1,0:T(8,12...) custom-call(s32[1]{0:T(128)} %bitcast.me, ...), custom_call_target="tpu_custom_call" | custom-call | flops 1610612736 | bytes 15728640 | tf_op jit(solution)/shard_map/pallas_call | solution.py:97
  249.9 1.4 collective-permute-start.24
  251.3 1.5 collective-permute-start.26
  252.8 1.2 collective-permute-start.30
  254.0 0.3 collective-permute-start.2
  254.2 15.4 %shard_map.111 = (bf16[16,128,128]{2,1,0:T(8,128)(2,1)}, bf16[16,128,128]{2,1,0:T(8,128)(2,1)}, bf16[16,128,128]{2,1,0:T(8,128)(2,1)}, bf16[16,128,128]{2,1,0:T(...) custom-call(s32[1]{0:T(128)} %bitcast.me, ...), custom_call_target="tpu_custom_call" | custom-call | flops 2147483648 | bytes 20971520 | tf_op jit(solution)/shard_map/pallas_call | solution.py:97
  269.7 1.3 collective-permute-start.15
  271.0 1.3 collective-permute-start.16
  272.3 1.0 collective-permute-start.32
  273.4 0.3 collective-permute-start.34
  273.7 2.1 collective-permute-start.36
  275.7 8.7 %collective-permute-done.32.refs_11_ = bf16[16,96,128]{2,1,0:T(8,128)(2,1)S(1)} collective-permute-done((bf16[16,96,128]{2,1,0:T(8,128)(2,1)}, bf16[16,96,128]{2,1,0:T(8,128)(2,1)S(1)}, u32[]{:S(2)}, u32[]{:S(2)}) %collective-permute-start.32) | collective-permute-done | bytes 393248 | tf_op jit(solution)/shard_map/ppermute | solution.py:359
  284.5 11.4 %collective-permute-done.34.refs_13_ = bf16[16,96,128]{2,1,0:T(8,128)(2,1)S(1)} collective-permute-done((bf16[16,96,128]{2,1,0:T(8,128)(2,1)}, bf16[16,96,128]{2,1,0:T(8,128)(2,1)S(1)}, u32[]{:S(2)}, u32[]{:S(2)}) %collective-permute-start.34) | collective-permute-done | bytes 393248 | tf_op jit(solution)/shard_map/ppermute | solution.py:359
  295.9 0.8 copy-done.11
  296.6 10.6 %collective-permute-done.36.refs_15_ = bf16[16,96,128]{2,1,0:T(8,128)(2,1)S(1)} collective-permute-done((bf16[16,96,128]{2,1,0:T(8,128)(2,1)}, bf16[16,96,128]{2,1,0:T(8,128)(2,1)S(1)}, u32[]{:S(2)}, u32[]{:S(2)}) %collective-permute-start.36) | collective-permute-done | bytes 393248 | tf_op jit(solution)/shard_map/ppermute | solution.py:359
  307.3 0.8 copy-done.13
  308.0 1.2 collective-permute-start.20
  309.3 0.9 copy.15.feed_of_slot
  310.2 0.7 copy-done.8
  310.9 3.9 %shard_map.110.refs_16_.refs_8_ = bf16[1088,1024]{1,0:T(8,128)(2,1)S(1)} custom-call(s32[1]{0:T(128)} %bitcast.me, s32[1024,1]{1,0:T(8,128)S(1)} %copy.15.feed_of_slot, f32[8,128]{1,0:T(8,128)S(1)} %copy-done.8), custom_call_target="tpu_custom_call" | custom-call | flops 41943040 | bytes 4194304 | tf_op jit(solution)/shard_map/pallas_call | solution.py:273
  314.8 1.0 copy-done.10
  315.8 1.0 copy-done.12
  316.8 1.0 copy-done.14
  317.8 0.9 copy-done.15
  318.7 0.9 copy-done.17
  319.6 0.9 copy-done.19
  320.5 7.9 %shard_map.115.refs_9_ = f32[1024,1024]{1,0:T(8,128)} custom-call(bf16[16,32,128]{2,1,0:T(8,128)(2,1)S(1)} %copy-done.15, bf16[16,96,128]{2,1,0:T(8,128)(2,1)S(1)} %copy-done.10, bf16[16,32,128]{2,1,0:T(8,128)(2,1)} %collective-permute-done.23.refs_2_, bf16[16,96,128]{2,1,0:T(8,128)(2,1)} %collective-permute-done.24.refs_3_, ...), custom_call_target="tpu_custom_call" | custom-call | flops 4294967296 | bytes 12582912 | tf_op jit(solution)/shard_map/pallas_call | solution.py:214
  328.4 3.9 %collective-permute-start.3 = (bf16[8,128,128]{2,1,0:T(8,128)(2,1)S(1)}, bf16[8,128,128]{2,1,0:T(8,128)(2,1)S(1)}, u32[]{:S(2)}, u32[]{:S(2)}) collective-permute-start(bf16[8,128,128]{2,1,0:T(8,128)(2,1)S(1)} %copy-done.24), channel_id=1, source_target_pairs={{0,3},{1,2},{2,1},{3,0},{4,7},{5,6},{6,5},{7,4},{8,11},{9,10},{10,... | collective-permute-start | bytes 786440 | tf_op jit(solution)/shard_map/ppermute | solution.py:359
  332.3 1.6 collective-permute-start.4
  333.9 2.6 collective-permute-done.19.refs_5_
  336.5 3.7 collective-permute-start.5
  340.1 13.9 %collective-permute-done.20.refs_6_ = bf16[16,128,128]{2,1,0:T(8,128)(2,1)} collective-permute-done((bf16[16,128,128]{2,1,0:T(8,128)(2,1)}, bf16[16,128,128]{2,1,0:T(8,128)(2,1)}, u32[]{:S(2)}, u32[]{:S(2)}) %collective-permute-start.20) | collective-permute-done | bytes 524320 | tf_op jit(solution)/shard_map/ppermute | solution.py:359
  354.0 1.2 collective-permute-start.6
  355.2 3.7 collective-permute-done.21.refs_7_
  358.9 2.8 collective-permute-start.7
  361.8 8.7 %shard_map.116.refs_9_ = f32[1024,1024]{1,0:T(8,128)} custom-call(bf16[16,128,128]{2,1,0:T(8,128)(2,1)S(1)} %copy-done.9, bf16[16,128,128]{2,1,0:T(8,128)(2,1)S(1)} %collective-permute-done.15.refs_1_, bf16[16,128,128]{2,1,0:T(8,128)(2,1)S(1)} %collective-permute-done.16.refs_2_, ...), custom_call_target="tpu_custom_call", output_to_operand_aliasing={{}: (9, {})} | custom-call | flops 4294967296 | bytes 12582912 | tf_op jit(solution)/shard_map/pallas_call | solution.py:214
  370.5 5.4 %shard_map.117.refs_9_ = f32[1024,1024]{1,0:T(8,128)} custom-call(bf16[8,128,128]{2,1,0:T(8,128)(2,1)S(1)} %copy-done.1, bf16[8,128,128]{2,1,0:T(8,128)(2,1)} %collective-permute-done.8.refs_1_, bf16[8,128,128]{2,1,0:T(8,128)(2,1)} %collective-permute-done.9.refs_2_, bf16[8,128,128]{2,1,0:T(8,128)(2,1)S(1)} %copy-done.3, ...), custom_call_target="tpu_custom_call", output_to_operand_aliasing={{}: (9, {})} | custom-call | flops 2147483648 | bytes 8388608 | tf_op jit(solution)/shard_map/pallas_call | solution.py:214
  375.9 5.2 %shard_map.118 = f32[1024,1024]{1,0:T(8,128)} custom-call(bf16[8,128,128]{2,1,0:T(8,128)(2,1)S(1)} %copy-done, bf16[8,128,128]{2,1,0:T(8,128)(2,1)} %collective-permute-done.1.refs_1_, bf16[8,128,128]{2,1,0:T(8,128)(2,1)} %collective-permute-done.2.refs_2_, bf16[8,128,128]{2,1,0:T(8,128)(2,1)S(1)} %collective-permute-done.3.refs_3_, ...), custom_call_target="tpu_custom_call", output_to_operand_aliasing={{}: (9, {})} | custom-call | flops 2147483648 | bytes 8388608 | tf_op jit(solution)/shard_map/pallas_call | solution.py:214
  (71 shorter events, 0.2 us)
Async XLA Ops:
  0.0 162.4 %collective-permute-start = (bf16[3,128,16384]{2,1,0:T(8,128)(2,1)}, bf16[3,128,16384]{2,1,0:T(8,128)(2,1)}, u32[]{:S(2)}, u32[]{:S(2)}) collective-permute-start(bf16[3,128,16384]{2,1,0:T(8,128)(2,1)} %v2.3), channel_id=1, source_target_pairs={{8,0},{16,8},{24,16},{9,1},{17,9},{25,17},{10,2},{18,10},{26,18},{... | collective-permute-start | bytes 37748744 | tf_op jit(solution)/shard_map/ppermute | solution.py:301
  4.6 146.9 %collective-permute-start.22 = (bf16[1,32,16384]{2,1,0:T(8,128)(2,1)}, bf16[1,32,16384]{2,1,0:T(8,128)(2,1)}, u32[]{:S(2)}, u32[]{:S(2)}) collective-permute-start(bf16[1,32,16384]{2,1,0:T(8,128)(2,1)} %shard_map.112), channel_id=1, source_target_pairs={{8,0},{16,8},{24,16},{9,1},{17,9},{25,17},{10,2},{18,10},{26,18},{... | collective-permute-start | bytes 3145736 | tf_op jit(solution)/shard_map/ppermute | solution.py:300
  157.3 20.9 %collective-permute-start.23 = (bf16[16,32,128]{2,1,0:T(8,128)(2,1)}, bf16[16,32,128]{2,1,0:T(8,128)(2,1)}, u32[]{:S(2)}, u32[]{:S(2)}) collective-permute-start(bf16[16,32,128]{2,1,0:T(8,128)(2,1)} %get-tuple-element.71), channel_id=1, source_target_pairs={{0,1},{1,0},{2,3},{3,2},{4,5},{5,4},{6,7},{7,6},{8,9},{9,8},{10,11... | collective-permute-start | bytes 393224 | tf_op jit(solution)/shard_map/ppermute | solution.py:359
  157.7 21.7 %collective-permute-start.25 = (bf16[16,32,128]{2,1,0:T(8,128)(2,1)}, bf16[16,32,128]{2,1,0:T(8,128)(2,1)}, u32[]{:S(2)}, u32[]{:S(2)}) collective-permute-start(bf16[16,32,128]{2,1,0:T(8,128)(2,1)} %get-tuple-element.73), channel_id=1, source_target_pairs={{0,2},{1,3},{2,0},{3,1},{4,6},{5,7},{6,4},{7,5},{8,10},{9,11},{10,... | collective-permute-start | bytes 393224 | tf_op jit(solution)/shard_map/ppermute | solution.py:359
  157.8 23.9 %collective-permute-start.27 = (bf16[16,32,128]{2,1,0:T(8,128)(2,1)}, bf16[16,32,128]{2,1,0:T(8,128)(2,1)}, u32[]{:S(2)}, u32[]{:S(2)}) collective-permute-start(bf16[16,32,128]{2,1,0:T(8,128)(2,1)} %get-tuple-element.75), channel_id=1, source_target_pairs={{0,3},{1,2},{2,1},{3,0},{4,7},{5,6},{6,5},{7,4},{8,11},{9,10},{10,... | collective-permute-start | bytes 393224 | tf_op jit(solution)/shard_map/ppermute | solution.py:359
  160.1 25.5 %collective-permute-start.29 = (bf16[16,32,128]{2,1,0:T(8,128)(2,1)}, bf16[16,32,128]{2,1,0:T(8,128)(2,1)}, u32[]{:S(2)}, u32[]{:S(2)}) collective-permute-start(bf16[16,32,128]{2,1,0:T(8,128)(2,1)} %get-tuple-element.77), channel_id=1, source_target_pairs={{0,4},{1,5},{2,6},{3,7},{4,0},{5,1},{6,2},{7,3},{8,12},{9,13},{10,... | collective-permute-start | bytes 393224 | tf_op jit(solution)/shard_map/ppermute | solution.py:359
  162.4 28.0 %collective-permute-start.31 = (bf16[16,32,128]{2,1,0:T(8,128)(2,1)}, bf16[16,32,128]{2,1,0:T(8,128)(2,1)}, u32[]{:S(2)}, u32[]{:S(2)}) collective-permute-start(bf16[16,32,128]{2,1,0:T(8,128)(2,1)} %get-tuple-element.79), channel_id=1, source_target_pairs={{0,5},{1,4},{2,7},{3,6},{4,1},{5,0},{6,3},{7,2},{8,13},{9,12},{10,... | collective-permute-start | bytes 393224 | tf_op jit(solution)/shard_map/ppermute | solution.py:359
  178.2 55.7 %collective-permute-start.10 = (bf16[8,128,128]{2,1,0:T(8,128)(2,1)}, bf16[8,128,128]{2,1,0:T(8,128)(2,1)S(1)}, u32[]{:S(2)}, u32[]{:S(2)}) collective-permute-start(bf16[8,128,128]{2,1,0:T(8,128)(2,1)} %get-tuple-element.56), channel_id=1, source_target_pairs={{0,3},{1,2},{2,1},{3,0},{4,7},{5,6},{6,5},{7,4},{8,11},{9,10},{10,... | collective-permute-start | bytes 786440 | tf_op jit(solution)/shard_map/ppermute | solution.py:359
  179.4 56.6 %collective-permute-start.11 = (bf16[8,128,128]{2,1,0:T(8,128)(2,1)}, bf16[8,128,128]{2,1,0:T(8,128)(2,1)S(1)}, u32[]{:S(2)}, u32[]{:S(2)}) collective-permute-start(bf16[8,128,128]{2,1,0:T(8,128)(2,1)} %get-tuple-element.57), channel_id=1, source_target_pairs={{0,4},{1,5},{2,6},{3,7},{4,0},{5,1},{6,2},{7,3},{8,12},{9,13},{10,... | collective-permute-start | bytes 786440 | tf_op jit(solution)/shard_map/ppermute | solution.py:359
  181.7 55.0 %collective-permute-start.12 = (bf16[8,128,128]{2,1,0:T(8,128)(2,1)}, bf16[8,128,128]{2,1,0:T(8,128)(2,1)S(1)}, u32[]{:S(2)}, u32[]{:S(2)}) collective-permute-start(bf16[8,128,128]{2,1,0:T(8,128)(2,1)} %get-tuple-element.58), channel_id=1, source_target_pairs={{0,5},{1,4},{2,7},{3,6},{4,1},{5,0},{6,3},{7,2},{8,13},{9,12},{10,... | collective-permute-start | bytes 786440 | tf_op jit(solution)/shard_map/ppermute | solution.py:359
  185.5 34.6 %collective-permute-start.33 = (bf16[16,32,128]{2,1,0:T(8,128)(2,1)}, bf16[16,32,128]{2,1,0:T(8,128)(2,1)S(1)}, u32[]{:S(2)}, u32[]{:S(2)}) collective-permute-start(bf16[16,32,128]{2,1,0:T(8,128)(2,1)} %get-tuple-element.81), channel_id=1, source_target_pairs={{0,6},{1,7},{2,4},{3,5},{4,2},{5,3},{6,0},{7,1},{8,14},{9,15},{10,... | collective-permute-start | bytes 393224 | tf_op jit(solution)/shard_map/ppermute | solution.py:359
  190.4 41.8 %collective-permute-start.35 = (bf16[16,32,128]{2,1,0:T(8,128)(2,1)}, bf16[16,32,128]{2,1,0:T(8,128)(2,1)S(1)}, u32[]{:S(2)}, u32[]{:S(2)}) collective-permute-start(bf16[16,32,128]{2,1,0:T(8,128)(2,1)} %get-tuple-element.83), channel_id=1, source_target_pairs={{0,7},{1,6},{2,5},{3,4},{4,3},{5,2},{6,1},{7,0},{8,15},{9,14},{10,... | collective-permute-start | bytes 393224 | tf_op jit(solution)/shard_map/ppermute | solution.py:359
  220.2 0.7 copy-start.16
  220.8 29.1 %collective-permute-start.13 = (bf16[8,128,128]{2,1,0:T(8,128)(2,1)}, bf16[8,128,128]{2,1,0:T(8,128)(2,1)}, u32[]{:S(2)}, u32[]{:S(2)}) collective-permute-start(bf16[8,128,128]{2,1,0:T(8,128)(2,1)} %get-tuple-element.59), channel_id=1, source_target_pairs={{0,6},{1,7},{2,4},{3,5},{4,2},{5,3},{6,0},{7,1},{8,14},{9,15},{10,... | collective-permute-start | bytes 786440 | tf_op jit(solution)/shard_map/ppermute | solution.py:359
  232.2 0.7 copy-start.18
  232.9 18.4 %collective-permute-start.14 = (bf16[8,128,128]{2,1,0:T(8,128)(2,1)}, bf16[8,128,128]{2,1,0:T(8,128)(2,1)}, u32[]{:S(2)}, u32[]{:S(2)}) collective-permute-start(bf16[8,128,128]{2,1,0:T(8,128)(2,1)} %get-tuple-element.60), channel_id=1, source_target_pairs={{0,7},{1,6},{2,5},{3,4},{4,3},{5,2},{6,1},{7,0},{8,15},{9,14},{10,... | collective-permute-start | bytes 786440 | tf_op jit(solution)/shard_map/ppermute | solution.py:359
  234.0 0.7 copy-start.2
  234.7 18.0 %collective-permute-start.8 = (bf16[8,128,128]{2,1,0:T(8,128)(2,1)}, bf16[8,128,128]{2,1,0:T(8,128)(2,1)}, u32[]{:S(2)}, u32[]{:S(2)}) collective-permute-start(bf16[8,128,128]{2,1,0:T(8,128)(2,1)} %get-tuple-element.54), channel_id=1, source_target_pairs={{0,1},{1,0},{2,3},{3,2},{4,5},{5,4},{6,7},{7,6},{8,9},{9,8},{10,11... | collective-permute-start | bytes 786440 | tf_op jit(solution)/shard_map/ppermute | solution.py:359
  236.0 0.7 copy-start.4
  236.7 16.0 %collective-permute-start.9 = (bf16[8,128,128]{2,1,0:T(8,128)(2,1)}, bf16[8,128,128]{2,1,0:T(8,128)(2,1)}, u32[]{:S(2)}, u32[]{:S(2)}) collective-permute-start(bf16[8,128,128]{2,1,0:T(8,128)(2,1)} %get-tuple-element.55), channel_id=1, source_target_pairs={{0,2},{1,3},{2,0},{3,1},{4,6},{5,7},{6,4},{7,5},{8,10},{9,11},{10,... | collective-permute-start | bytes 786440 | tf_op jit(solution)/shard_map/ppermute | solution.py:359
  236.7 0.7 copy-start.6
  237.5 16.5 %collective-permute-start.1 = (bf16[8,128,128]{2,1,0:T(8,128)(2,1)}, bf16[8,128,128]{2,1,0:T(8,128)(2,1)}, u32[]{:S(2)}, u32[]{:S(2)}) collective-permute-start(bf16[8,128,128]{2,1,0:T(8,128)(2,1)} %get-tuple-element.46), channel_id=1, source_target_pairs={{0,1},{1,0},{2,3},{3,2},{4,5},{5,4},{6,7},{7,6},{8,9},{9,8},{10,11... | collective-permute-start | bytes 786440 | tf_op jit(solution)/shard_map/ppermute | solution.py:359
  249.9 21.1 %collective-permute-start.24 = (bf16[16,96,128]{2,1,0:T(8,128)(2,1)}, bf16[16,96,128]{2,1,0:T(8,128)(2,1)}, u32[]{:S(2)}, u32[]{:S(2)}) collective-permute-start(bf16[16,96,128]{2,1,0:T(8,128)(2,1)} %get-tuple-element.72), channel_id=1, source_target_pairs={{0,1},{1,0},{2,3},{3,2},{4,5},{5,4},{6,7},{7,6},{8,9},{9,8},{10,11... | collective-permute-start | bytes 1179656 | tf_op jit(solution)/shard_map/ppermute | solution.py:359
  251.3 21.1 %collective-permute-start.26 = (bf16[16,96,128]{2,1,0:T(8,128)(2,1)}, bf16[16,96,128]{2,1,0:T(8,128)(2,1)}, u32[]{:S(2)}, u32[]{:S(2)}) collective-permute-start(bf16[16,96,128]{2,1,0:T(8,128)(2,1)} %get-tuple-element.74), channel_id=1, source_target_pairs={{0,2},{1,3},{2,0},{3,1},{4,6},{5,7},{6,4},{7,5},{8,10},{9,11},{10,... | collective-permute-start | bytes 1179656 | tf_op jit(solution)/shard_map/ppermute | solution.py:359
  252.8 20.6 %collective-permute-start.28 = (bf16[16,96,128]{2,1,0:T(8,128)(2,1)}, bf16[16,96,128]{2,1,0:T(8,128)(2,1)}, u32[]{:S(2)}, u32[]{:S(2)}) collective-permute-start(bf16[16,96,128]{2,1,0:T(8,128)(2,1)} %get-tuple-element.76), channel_id=1, source_target_pairs={{0,3},{1,2},{2,1},{3,0},{4,7},{5,6},{6,5},{7,4},{8,11},{9,10},{10,... | collective-permute-start | bytes 1179656 | tf_op jit(solution)/shard_map/ppermute | solution.py:359
  252.8 20.9 %collective-permute-start.30 = (bf16[16,96,128]{2,1,0:T(8,128)(2,1)}, bf16[16,96,128]{2,1,0:T(8,128)(2,1)}, u32[]{:S(2)}, u32[]{:S(2)}) collective-permute-start(bf16[16,96,128]{2,1,0:T(8,128)(2,1)} %get-tuple-element.78), channel_id=1, source_target_pairs={{0,4},{1,5},{2,6},{3,7},{4,0},{5,1},{6,2},{7,3},{8,12},{9,13},{10,... | collective-permute-start | bytes 1179656 | tf_op jit(solution)/shard_map/ppermute | solution.py:359
  254.0 15.7 %collective-permute-start.2 = (bf16[8,128,128]{2,1,0:T(8,128)(2,1)}, bf16[8,128,128]{2,1,0:T(8,128)(2,1)}, u32[]{:S(2)}, u32[]{:S(2)}) collective-permute-start(bf16[8,128,128]{2,1,0:T(8,128)(2,1)} %get-tuple-element.47), channel_id=1, source_target_pairs={{0,2},{1,3},{2,0},{3,1},{4,6},{5,7},{6,4},{7,5},{8,10},{9,11},{10,... | collective-permute-start | bytes 786440 | tf_op jit(solution)/shard_map/ppermute | solution.py:359
  269.7 38.3 %collective-permute-start.15 = (bf16[16,128,128]{2,1,0:T(8,128)(2,1)}, bf16[16,128,128]{2,1,0:T(8,128)(2,1)S(1)}, u32[]{:S(2)}, u32[]{:S(2)}) collective-permute-start(bf16[16,128,128]{2,1,0:T(8,128)(2,1)} %get-tuple-element.62), channel_id=1, source_target_pairs={{0,1},{1,0},{2,3},{3,2},{4,5},{5,4},{6,7},{7,6},{8,9},{9,8},{10,11... | collective-permute-start | bytes 1572872 | tf_op jit(solution)/shard_map/ppermute | solution.py:359
  271.0 38.3 %collective-permute-start.16 = (bf16[16,128,128]{2,1,0:T(8,128)(2,1)}, bf16[16,128,128]{2,1,0:T(8,128)(2,1)S(1)}, u32[]{:S(2)}, u32[]{:S(2)}) collective-permute-start(bf16[16,128,128]{2,1,0:T(8,128)(2,1)} %get-tuple-element.63), channel_id=1, source_target_pairs={{0,2},{1,3},{2,0},{3,1},{4,6},{5,7},{6,4},{7,5},{8,10},{9,11},{10,... | collective-permute-start | bytes 1572872 | tf_op jit(solution)/shard_map/ppermute | solution.py:359
  272.3 12.1 %collective-permute-start.32 = (bf16[16,96,128]{2,1,0:T(8,128)(2,1)}, bf16[16,96,128]{2,1,0:T(8,128)(2,1)S(1)}, u32[]{:S(2)}, u32[]{:S(2)}) collective-permute-start(bf16[16,96,128]{2,1,0:T(8,128)(2,1)} %get-tuple-element.80), channel_id=1, source_target_pairs={{0,5},{1,4},{2,7},{3,6},{4,1},{5,0},{6,3},{7,2},{8,13},{9,12},{10,... | collective-permute-start | bytes 1179656 | tf_op jit(solution)/shard_map/ppermute | solution.py:359
  273.4 22.5 %collective-permute-start.34 = (bf16[16,96,128]{2,1,0:T(8,128)(2,1)}, bf16[16,96,128]{2,1,0:T(8,128)(2,1)S(1)}, u32[]{:S(2)}, u32[]{:S(2)}) collective-permute-start(bf16[16,96,128]{2,1,0:T(8,128)(2,1)} %get-tuple-element.82), channel_id=1, source_target_pairs={{0,6},{1,7},{2,4},{3,5},{4,2},{5,3},{6,0},{7,1},{8,14},{9,15},{10,... | collective-permute-start | bytes 1179656 | tf_op jit(solution)/shard_map/ppermute | solution.py:359
  273.7 33.6 %collective-permute-start.36 = (bf16[16,96,128]{2,1,0:T(8,128)(2,1)}, bf16[16,96,128]{2,1,0:T(8,128)(2,1)S(1)}, u32[]{:S(2)}, u32[]{:S(2)}) collective-permute-start(bf16[16,96,128]{2,1,0:T(8,128)(2,1)} %get-tuple-element.84), channel_id=1, source_target_pairs={{0,7},{1,6},{2,5},{3,4},{4,3},{5,2},{6,1},{7,0},{8,15},{9,14},{10,... | collective-permute-start | bytes 1179656 | tf_op jit(solution)/shard_map/ppermute | solution.py:359
  284.5 43.9 %collective-permute-start.17 = (bf16[16,128,128]{2,1,0:T(8,128)(2,1)}, bf16[16,128,128]{2,1,0:T(8,128)(2,1)S(1)}, u32[]{:S(2)}, u32[]{:S(2)}) collective-permute-start(bf16[16,128,128]{2,1,0:T(8,128)(2,1)} %get-tuple-element.64), channel_id=1, source_target_pairs={{0,3},{1,2},{2,1},{3,0},{4,7},{5,6},{6,5},{7,4},{8,11},{9,10},{10,... | collective-permute-start | bytes 1572872 | tf_op jit(solution)/shard_map/ppermute | solution.py:359
  295.9 0.8 copy-start.11
  296.6 35.6 %collective-permute-start.18 = (bf16[16,128,128]{2,1,0:T(8,128)(2,1)}, bf16[16,128,128]{2,1,0:T(8,128)(2,1)S(1)}, u32[]{:S(2)}, u32[]{:S(2)}) collective-permute-start(bf16[16,128,128]{2,1,0:T(8,128)(2,1)} %get-tuple-element.65), channel_id=1, source_target_pairs={{0,4},{1,5},{2,6},{3,7},{4,0},{5,1},{6,2},{7,3},{8,12},{9,13},{10,... | collective-permute-start | bytes 1572872 | tf_op jit(solution)/shard_map/ppermute | solution.py:359
  307.3 0.8 copy-start.13
  308.0 28.4 %collective-permute-start.19 = (bf16[16,128,128]{2,1,0:T(8,128)(2,1)}, bf16[16,128,128]{2,1,0:T(8,128)(2,1)S(1)}, u32[]{:S(2)}, u32[]{:S(2)}) collective-permute-start(bf16[16,128,128]{2,1,0:T(8,128)(2,1)} %get-tuple-element.66), channel_id=1, source_target_pairs={{0,5},{1,4},{2,7},{3,6},{4,1},{5,0},{6,3},{7,2},{8,13},{9,12},{10,... | collective-permute-start | bytes 1572872 | tf_op jit(solution)/shard_map/ppermute | solution.py:359
  308.0 46.0 %collective-permute-start.20 = (bf16[16,128,128]{2,1,0:T(8,128)(2,1)}, bf16[16,128,128]{2,1,0:T(8,128)(2,1)}, u32[]{:S(2)}, u32[]{:S(2)}) collective-permute-start(bf16[16,128,128]{2,1,0:T(8,128)(2,1)} %get-tuple-element.67), channel_id=1, source_target_pairs={{0,6},{1,7},{2,4},{3,5},{4,2},{5,3},{6,0},{7,1},{8,14},{9,15},{10,... | collective-permute-start | bytes 1572872 | tf_op jit(solution)/shard_map/ppermute | solution.py:359
  309.3 49.7 %collective-permute-start.21 = (bf16[16,128,128]{2,1,0:T(8,128)(2,1)}, bf16[16,128,128]{2,1,0:T(8,128)(2,1)}, u32[]{:S(2)}, u32[]{:S(2)}) collective-permute-start(bf16[16,128,128]{2,1,0:T(8,128)(2,1)} %get-tuple-element.68), channel_id=1, source_target_pairs={{0,7},{1,6},{2,5},{3,4},{4,3},{5,2},{6,1},{7,0},{8,15},{9,14},{10,... | collective-permute-start | bytes 1572872 | tf_op jit(solution)/shard_map/ppermute | solution.py:359
  310.2 0.7 copy-start.8
  314.8 1.0 copy-start.10
  315.8 1.0 copy-start.12
  316.8 1.0 copy-start.14
  317.8 0.9 copy-start.15
  318.7 0.9 copy-start.17
  319.6 0.9 copy-start.19
  320.5 7.9 %copy-start.24 = (bf16[8,128,128]{2,1,0:T(8,128)(2,1)S(1)}, bf16[8,128,128]{2,1,0:T(8,128)(2,1)}, u32[]{:S(2)}) copy-start(bf16[8,128,128]{2,1,0:T(8,128)(2,1)} %get-tuple-element.48) | copy-start | bytes 786436
  320.5 11.8 %copy-start.23 = (bf16[8,128,128]{2,1,0:T(8,128)(2,1)S(1)}, bf16[8,128,128]{2,1,0:T(8,128)(2,1)}, u32[]{:S(2)}) copy-start(bf16[8,128,128]{2,1,0:T(8,128)(2,1)} %get-tuple-element.49) | copy-start | bytes 786436
  320.5 16.0 %copy-start.22 = (bf16[8,128,128]{2,1,0:T(8,128)(2,1)S(1)}, bf16[8,128,128]{2,1,0:T(8,128)(2,1)}, u32[]{:S(2)}) copy-start(bf16[8,128,128]{2,1,0:T(8,128)(2,1)} %get-tuple-element.50) | copy-start | bytes 786436
  320.5 33.5 %copy-start.21 = (bf16[8,128,128]{2,1,0:T(8,128)(2,1)S(1)}, bf16[8,128,128]{2,1,0:T(8,128)(2,1)}, u32[]{:S(2)}) copy-start(bf16[8,128,128]{2,1,0:T(8,128)(2,1)} %get-tuple-element.51) | copy-start | bytes 786436
  320.5 38.4 %copy-start.20 = (bf16[8,128,128]{2,1,0:T(8,128)(2,1)S(1)}, bf16[8,128,128]{2,1,0:T(8,128)(2,1)}, u32[]{:S(2)}) copy-start(bf16[8,128,128]{2,1,0:T(8,128)(2,1)} %get-tuple-element.52) | copy-start | bytes 786436
  320.5 41.2 %copy-start.9 = (bf16[16,128,128]{2,1,0:T(8,128)(2,1)S(1)}, bf16[16,128,128]{2,1,0:T(8,128)(2,1)}, u32[]{:S(2)}) copy-start(bf16[16,128,128]{2,1,0:T(8,128)(2,1)} %get-tuple-element.61.refs_0_) | copy-start | bytes 1572868
  328.4 47.4 %collective-permute-start.3 = (bf16[8,128,128]{2,1,0:T(8,128)(2,1)S(1)}, bf16[8,128,128]{2,1,0:T(8,128)(2,1)S(1)}, u32[]{:S(2)}, u32[]{:S(2)}) collective-permute-start(bf16[8,128,128]{2,1,0:T(8,128)(2,1)S(1)} %copy-done.24), channel_id=1, source_target_pairs={{0,3},{1,2},{2,1},{3,0},{4,7},{5,6},{6,5},{7,4},{8,11},{9,10},{10,... | collective-permute-start | bytes 786440 | tf_op jit(solution)/shard_map/ppermute | solution.py:359
  332.3 43.6 %collective-permute-start.4 = (bf16[8,128,128]{2,1,0:T(8,128)(2,1)S(1)}, bf16[8,128,128]{2,1,0:T(8,128)(2,1)S(1)}, u32[]{:S(2)}, u32[]{:S(2)}) collective-permute-start(bf16[8,128,128]{2,1,0:T(8,128)(2,1)S(1)} %copy-done.23), channel_id=1, source_target_pairs={{0,4},{1,5},{2,6},{3,7},{4,0},{5,1},{6,2},{7,3},{8,12},{9,13},{10,... | collective-permute-start | bytes 786440 | tf_op jit(solution)/shard_map/ppermute | solution.py:359
  336.5 39.4 %collective-permute-start.5 = (bf16[8,128,128]{2,1,0:T(8,128)(2,1)S(1)}, bf16[8,128,128]{2,1,0:T(8,128)(2,1)S(1)}, u32[]{:S(2)}, u32[]{:S(2)}) collective-permute-start(bf16[8,128,128]{2,1,0:T(8,128)(2,1)S(1)} %copy-done.22), channel_id=1, source_target_pairs={{0,5},{1,4},{2,7},{3,6},{4,1},{5,0},{6,3},{7,2},{8,13},{9,12},{10,... | collective-permute-start | bytes 786440 | tf_op jit(solution)/shard_map/ppermute | solution.py:359
  354.0 21.9 %collective-permute-start.6 = (bf16[8,128,128]{2,1,0:T(8,128)(2,1)S(1)}, bf16[8,128,128]{2,1,0:T(8,128)(2,1)S(1)}, u32[]{:S(2)}, u32[]{:S(2)}) collective-permute-start(bf16[8,128,128]{2,1,0:T(8,128)(2,1)S(1)} %copy-done.21), channel_id=1, source_target_pairs={{0,6},{1,7},{2,4},{3,5},{4,2},{5,3},{6,0},{7,1},{8,14},{9,15},{10,... | collective-permute-start | bytes 786440 | tf_op jit(solution)/shard_map/ppermute | solution.py:359
  358.9 16.9 %collective-permute-start.7 = (bf16[8,128,128]{2,1,0:T(8,128)(2,1)S(1)}, bf16[8,128,128]{2,1,0:T(8,128)(2,1)S(1)}, u32[]{:S(2)}, u32[]{:S(2)}) collective-permute-start(bf16[8,128,128]{2,1,0:T(8,128)(2,1)S(1)} %copy-done.20), channel_id=1, source_target_pairs={{0,7},{1,6},{2,5},{3,4},{4,3},{5,2},{6,1},{7,0},{8,15},{9,14},{10,... | collective-permute-start | bytes 786440 | tf_op jit(solution)/shard_map/ppermute | solution.py:359
  361.8 8.7 %copy-start.1 = (bf16[8,128,128]{2,1,0:T(8,128)(2,1)S(1)}, bf16[8,128,128]{2,1,0:T(8,128)(2,1)}, u32[]{:S(2)}) copy-start(bf16[8,128,128]{2,1,0:T(8,128)(2,1)} %get-tuple-element.53.refs_0_) | copy-start | bytes 786436
  361.8 8.7 %copy-start.3 = (bf16[8,128,128]{2,1,0:T(8,128)(2,1)S(1)}, bf16[8,128,128]{2,1,0:T(8,128)(2,1)}, u32[]{:S(2)}) copy-start(bf16[8,128,128]{2,1,0:T(8,128)(2,1)} %copy-done.2) | copy-start | bytes 786436
  361.8 8.7 %copy-start.5 = (bf16[8,128,128]{2,1,0:T(8,128)(2,1)S(1)}, bf16[8,128,128]{2,1,0:T(8,128)(2,1)}, u32[]{:S(2)}) copy-start(bf16[8,128,128]{2,1,0:T(8,128)(2,1)} %copy-done.4) | copy-start | bytes 786436
  361.8 8.7 %copy-start.7 = (bf16[8,128,128]{2,1,0:T(8,128)(2,1)S(1)}, bf16[8,128,128]{2,1,0:T(8,128)(2,1)}, u32[]{:S(2)}) copy-start(bf16[8,128,128]{2,1,0:T(8,128)(2,1)} %copy-done.6) | copy-start | bytes 786436
  370.4 5.4 %copy-start = (bf16[8,128,128]{2,1,0:T(8,128)(2,1)S(1)}, bf16[8,128,128]{2,1,0:T(8,128)(2,1)}, u32[]{:S(2)}) copy-start(bf16[8,128,128]{2,1,0:T(8,128)(2,1)} %get-tuple-element.45.refs_0_) | copy-start | bytes 786436
